TPU v7x, 256 devices: a whole 4x4x8 slice. The times are simulated.
256 devices in a mesh: row: 16 (over x_lo, z), col: 16 (over x_hi, y, core).
Axes of the slice: x: 4 (x_hi: 2, x_lo: 2; x = x_hi * 2 + x_lo), y: 4, z: 8, core: 2. Of those that a mesh axis runs over, the one named last changes fastest.
Arguments:
- features: bfloat16 [32768, 1024], P(('row', 'col')), may hold values from -6 to 6
- weight: bfloat16 [1024, 1024], replicated, may hold values from -0.1875 to 0.1875
- cotangent: bfloat16 [32768, 1024], P(('col', 'row')), may hold values from -6 to 6
- tile_values: bfloat16 [16, 16, 64, 128, 128], P('row', 'col'), may hold values from -0.1875 to 0.1875
- block_row: int32 [16, 16, 64], P('row', 'col'), may hold values from 0 to 15, as said below
- block_column: int32 [16, 16, 64], P('row', 'col'), may hold values from 0 to 15, as said below
- tile_count: int32 [16, 16], P('row', 'col'), may hold values from 16 to 64, as said below
Outputs:
- activated: bfloat16 [32768, 1024], P(('col', 'row'))
- feat_grad: bfloat16 [32768, 1024], P(('row', 'col'))
- weight_grad: float32 [1024, 1024], replicated
Inputs may be any that keep to these rules, and one draw needn't show every extreme that they name: `block_row`: within one grid position the slots name distinct region cells. `block_column`: within one grid position the slots name distinct region cells. `tile_count`: some grid position has exactly 64 live slots.
All inputs are finite; a program needn't handle non-finite values.
Results may differ from a plain program's by a relative error of at most 0.02.
Values may be sent and summed in bfloat16 or wider, within the bound.
A program may use at most 128 MiB of HBM per device.

v0:
```python
import jax
import jax.numpy as jnp
from jax import lax
from jax.sharding import PartitionSpec as P


def silu_slope(hidden):
    sigmoid = jax.nn.sigmoid(hidden)
    return sigmoid * (1.0 + hidden * (1.0 - sigmoid))


def spread_tiles(source, tile_block, index_in, index_out, live_count, out_blocks, flipped):
    block_size = tile_block.shape[-1]
    width = source.shape[-1]
    blocks = source.reshape(-1, block_size, width)
    per_turn = 16
    form = "tba,tbf->taf" if flipped else "tab,tbf->taf"

    def add_turn(turn, summed):
        first = turn * per_turn
        matrix = lax.dynamic_slice_in_dim(tile_block, first, per_turn, 0)
        wanted = lax.dynamic_slice_in_dim(index_in, first, per_turn, 0)
        placed = lax.dynamic_slice_in_dim(index_out, first, per_turn, 0)
        is_live = first + jnp.arange(per_turn, dtype=jnp.int32) < live_count
        picked = blocks[wanted]
        products = jnp.einsum(form, matrix, picked, preferred_element_type=jnp.float32)
        products = products * is_live.astype(jnp.float32)[:, None, None]
        return summed.at[placed].add(products)

    turns = (live_count + per_turn - 1) // per_turn
    summed = lax.fori_loop(
        0, turns, add_turn, jnp.zeros((out_blocks, block_size, width), jnp.float32)
    )
    return summed.reshape(out_blocks * block_size, width)


def on_device(features, weight, cotangent, tile_values, block_row, block_column, tile_count):
    row_devices = lax.axis_size("row")
    col_devices = lax.axis_size("col")
    span = features.shape[0]
    block_size = tile_values.shape[-1]
    per_device = span // block_size
    tile_block = tile_values[0, 0]
    rows_index = block_row[0, 0]
    cols_index = block_column[0, 0]
    live_count = tile_count[0, 0]
    projected = jnp.dot(features, weight, preferred_element_type=jnp.float32).astype(jnp.bfloat16)
    gathered = lax.all_gather(projected, "col", axis=0, tiled=True)
    partial_value = spread_tiles(
        gathered, tile_block, cols_index, rows_index, live_count, row_devices * per_device, False
    )
    hidden = lax.psum_scatter(
        partial_value.astype(jnp.bfloat16), "row", scatter_dimension=0, tiled=True
    ).astype(jnp.float32)
    activated = jax.nn.silu(hidden).astype(jnp.bfloat16)
    hidden_grad = (cotangent.astype(jnp.float32) * silu_slope(hidden)).astype(jnp.bfloat16)
    grad_group = lax.all_gather(hidden_grad, "row", axis=0, tiled=True)
    back_partial = spread_tiles(
        grad_group, tile_block, rows_index, cols_index, live_count, col_devices * per_device, True
    )
    feat_delta = lax.psum_scatter(
        back_partial.astype(jnp.bfloat16), "col", scatter_dimension=0, tiled=True
    )
    feat_grad = jnp.dot(feat_delta, weight.T, preferred_element_type=jnp.float32).astype(
        jnp.bfloat16
    )
    weight_terms = lax.dot_general(
        features, feat_delta, (((0,), (0,)), ((), ())), preferred_element_type=jnp.float32
    )
    factor = (span * row_devices * col_devices) ** (-0.5)
    weight_grad = lax.psum(weight_terms, ("row", "col")) * factor
    return (activated, feat_grad, weight_grad)


def solution(mesh):
    return jax.shard_map(
        on_device,
        mesh=mesh,
        in_specs=(
            P(("row", "col"), None),
            P(),
            P(("col", "row"), None),
            P("row", "col", None, None, None),
            P("row", "col", None),
            P("row", "col", None),
            P("row", "col"),
        ),
        out_specs=(P(("col", "row"), None), P(("row", "col"), None), P()),
        check_vma=False,
    )
```

profile of v0, /device:TPU:1, one launch (start us, length us, event | category | flops | bytes accessed | tf_op | source)
XLA Modules:
  0.0 872.6 jit_solution(16505086763936700742)
XLA Ops:
  7.2 1.5 copy-done
  8.8 2.1 convolution_convert_fusion.1
  11.6 63.8 %all-gather.3.cloned.1.call-done = bf16[2048,1024]{1,0:T(8,128)(2,1)} async-done(((bf16[128,1024]{1,0:T(8,128)(2,1)}), bf16[2048,1024]{1,0:T(8,128)(2,1)}) %all-gather.3.cloned.1.call-update) | async-done | bytes 4194320 | tf_op jit(solution)/shard_map/all_gather | solution.py:48
  75.4 4.3 broadcast.35.clone
  79.7 92.0 %while.20 = (s32[]{:T(128)}, f32[16,128,1024]{2,1,0:T(8,128)}, s32[]{:T(128)}, s32[64]{0:T(128)S(1)}, bf16[64,128,128]{2,1,0:T(8,128)(2,1)}, /*index=5*/s32[64]{...) while((s32[]{:T(128)}, f32[16,128,1024]{2,1,0:T(8,128)}, ...), condition=%wide.region_2.3_spmd, body=%wide.region_0.2_spmd.sunk | while | flops 541066368 | bytes 46666480 | solution.py:31
  79.7 0.6 compare_convert_fusion.4
  80.4 0.1 compare_select_fusion.6
  80.5 5.0 gather_fusion
  85.5 6.8 broadcast_multiply_fusion.5
  92.3 18.0 %scatter_fusion = f32[16,128,1024]{2,1,0:T(8,128)} fusion(f32[16,128,1024]{2,1,0:T(8,128)} %get-tuple-element.261, s32[16]{0:T(128)S(1)} %get-tuple-element.236, f32[16,128,1024]{2,1,0:T(8,128)} %broadcast_multiply_fusion.5), kind=kCustom, calls=%fused_computation.2.clone.1 | custom fusion | flops 2097152 | bytes 25165888 | tf_op jit(solution)/shard_map/while/body/scatter-add | solution.py:28
  110.3 0.6 compare_convert_fusion.4
  111.0 0.1 compare_select_fusion.6
  111.0 5.0 gather_fusion
  116.1 6.8 broadcast_multiply_fusion.5
  122.9 18.2 %scatter_fusion = f32[16,128,1024]{2,1,0:T(8,128)} fusion(f32[16,128,1024]{2,1,0:T(8,128)} %get-tuple-element.261, s32[16]{0:T(128)S(1)} %get-tuple-element.236, f32[16,128,1024]{2,1,0:T(8,128)} %broadcast_multiply_fusion.5), kind=kCustom, calls=%fused_computation.2.clone.1 | custom fusion | flops 2097152 | bytes 25165888 | tf_op jit(solution)/shard_map/while/body/scatter-add | solution.py:28
  141.1 0.6 compare_convert_fusion.4
  141.8 0.1 compare_select_fusion.6
  141.8 5.0 gather_fusion
  146.9 6.8 broadcast_multiply_fusion.5
  153.7 18.0 %scatter_fusion = f32[16,128,1024]{2,1,0:T(8,128)} fusion(f32[16,128,1024]{2,1,0:T(8,128)} %get-tuple-element.261, s32[16]{0:T(128)S(1)} %get-tuple-element.236, f32[16,128,1024]{2,1,0:T(8,128)} %broadcast_multiply_fusion.5), kind=kCustom, calls=%fused_computation.2.clone.1 | custom fusion | flops 2097152 | bytes 25165888 | tf_op jit(solution)/shard_map/while/body/scatter-add | solution.py:28
  171.7 6.1 convert_element_type.45
  177.8 98.7 %reduce-scatter.3.cloned.1.call-done = bf16[128,1024]{1,0:T(8,128)(2,1)} async-done(((bf16[2048,1024]{1,0:T(8,128)(2,1)}), bf16[128,1024]{1,0:T(8,128)(2,1)}) %reduce-scatter.3.cloned.1.call-update) | async-done | bytes 262160 | tf_op jit(solution)/shard_map/reduce_scatter | solution.py:52
  276.5 2.0 fusion.11
  278.6 4.1 copy.10
  282.7 70.5 %all-gather.5.cloned.1.call-done = bf16[2048,1024]{1,0:T(8,128)(2,1)} async-done(((bf16[128,1024]{1,0:T(8,128)(2,1)}), bf16[2048,1024]{1,0:T(8,128)(2,1)}) %all-gather.5.cloned.1.call-update) | async-done | bytes 4194320 | tf_op jit(solution)/shard_map/all_gather | solution.py:57
  353.1 4.3 broadcast.35
  357.4 92.4 %while.21 = (s32[]{:T(128)}, f32[16,128,1024]{2,1,0:T(8,128)}, s32[]{:T(128)}, s32[64]{0:T(128)S(1)}, bf16[64,128,128]{1,2,0:T(8,128)(2,1)}, /*index=5*/s32[64]{...) while((s32[]{:T(128)}, f32[16,128,1024]{2,1,0:T(8,128)}, ...), condition=%wide.region_6.7_spmd, body=%wide.region_4.6_spmd.sunk | while | flops 541066368 | bytes 46666480 | solution.py:31
  357.4 0.6 compare_convert_fusion.5
  358.0 0.1 compare_select_fusion.7
  358.1 5.0 gather_fusion.1
  363.2 6.8 broadcast_multiply_fusion.6
  370.0 18.1 %scatter_fusion.1 = f32[16,128,1024]{2,1,0:T(8,128)} fusion(f32[16,128,1024]{2,1,0:T(8,128)} %get-tuple-element.297, s32[16]{0:T(128)S(1)} %get-tuple-element.246, f32[16,128,1024]{2,1,0:T(8,128)} %broadcast_multiply_fusion.6), kind=kCustom, calls=%fused_computation.3.clone.1 | custom fusion | flops 2097152 | bytes 25165888 | tf_op jit(solution)/shard_map/while/body/scatter-add | solution.py:28
  388.1 0.6 compare_convert_fusion.5
  388.8 0.1 compare_select_fusion.7
  388.9 5.0 gather_fusion.1
  393.9 6.8 broadcast_multiply_fusion.6
  400.7 18.2 %scatter_fusion.1 = f32[16,128,1024]{2,1,0:T(8,128)} fusion(f32[16,128,1024]{2,1,0:T(8,128)} %get-tuple-element.297, s32[16]{0:T(128)S(1)} %get-tuple-element.246, f32[16,128,1024]{2,1,0:T(8,128)} %broadcast_multiply_fusion.6), kind=kCustom, calls=%fused_computation.3.clone.1 | custom fusion | flops 2097152 | bytes 25165888 | tf_op jit(solution)/shard_map/while/body/scatter-add | solution.py:28
  418.9 0.6 compare_convert_fusion.5
  419.7 5.0 gather_fusion.1
  424.7 6.8 broadcast_multiply_fusion.6
  431.5 18.3 %scatter_fusion.1 = f32[16,128,1024]{2,1,0:T(8,128)} fusion(f32[16,128,1024]{2,1,0:T(8,128)} %get-tuple-element.297, s32[16]{0:T(128)S(1)} %get-tuple-element.246, f32[16,128,1024]{2,1,0:T(8,128)} %broadcast_multiply_fusion.6), kind=kCustom, calls=%fused_computation.3.clone.1 | custom fusion | flops 2097152 | bytes 25165888 | tf_op jit(solution)/shard_map/while/body/scatter-add | solution.py:28
  449.8 6.1 convert_element_type.51
  456.0 125.0 %reduce-scatter.5.cloned.1.call-done = bf16[128,1024]{1,0:T(8,128)(2,1)} async-done(((bf16[2048,1024]{1,0:T(8,128)(2,1)}), bf16[128,1024]{1,0:T(8,128)(2,1)}) %reduce-scatter.5.cloned.1.call-update) | async-done | bytes 262160 | tf_op jit(solution)/shard_map/reduce_scatter | solution.py:61
  580.9 3.8 convolution_bitcast_fusion
  584.7 1.5 convolution_convert_fusion
  586.3 269.4 %all-reduce.2.cloned.1.call-done = f32[1024,1024]{0,1:T(8,128)} async-done(((f32[1024,1024]{0,1:T(8,128)}), f32[1024,1024]{0,1:T(8,128)}) %all-reduce.2.cloned.1.call-update) | async-done | bytes 4194320 | tf_op jit(solution)/shard_map/psum | solution.py:71
  855.7 5.1 broadcast_multiply_fusion.2
  860.7 5.3 copy.12
  (28 shorter events, 0.4 us)
Async XLA Ops:
  7.2 1.6 copy-start
  7.2 68.2 %all-gather.3.cloned.1.call-start = ((), (), s32[]{:S(2)}) async-start(), calls=%async_computation.2 | async-start | bytes 4456448 | tf_op jit(solution)/shard_map/all_gather | solution.py:48
  10.9 265.6 %reduce-scatter.3.cloned.1.call-start = ((), (), s32[]{:S(2)}) async-start(), calls=%async_computation.3 | async-start | bytes 4456448 | tf_op jit(solution)/shard_map/reduce_scatter | solution.py:52
  75.4 4.3 copy-start.4
  75.4 4.3 copy-start.5
  177.7 98.8 %copy-start.3 = (bf16[128,1024]{1,0:T(8,128)(2,1)S(1)}, bf16[128,1024]{1,0:T(8,128)(2,1)}, u32[]{:S(2)}) copy-start(bf16[128,1024]{1,0:T(8,128)(2,1)} %param.13) | copy-start | bytes 786436
  177.8 175.3 %all-gather.5.cloned.1.call-start = ((), (), s32[]{:S(2)}) async-start(), calls=%async_computation.4 | async-start | bytes 4456448 | tf_op jit(solution)/shard_map/all_gather | solution.py:57
  278.5 302.4 %reduce-scatter.5.cloned.1.call-start = ((), (), s32[]{:S(2)}) async-start(), calls=%async_computation.5 | async-start | bytes 4456448 | tf_op jit(solution)/shard_map/reduce_scatter | solution.py:61
  455.9 125.0 %copy-start.1 = (bf16[128,1024]{1,0:T(8,128)(2,1)S(1)}, bf16[128,1024]{1,0:T(8,128)(2,1)}, u32[]{:S(2)}) copy-start(bf16[128,1024]{1,0:T(8,128)(2,1)} %param.11) | copy-start | bytes 786436
  455.9 399.8 %all-reduce.2.cloned.1.call-start = ((), (), s32[]{:S(2)}) async-start(), calls=%async_computation.6 | async-start | bytes 8388608 | tf_op jit(solution)/shard_map/psum | solution.py:71
  580.9 3.8 copy-start.2
Sparse Core Ops, SparseCore 0:
  11.3 64.0 all-gather.2
  177.9 98.5 reduce-scatter.2
  278.9 74.1 all-gather.4
  456.0 124.8 reduce-scatter.4
  586.8 268.8 all-reduce.1
where the time goes:
time: 875 us; the launch traced here: 873 us
  waiting for transfers between devices  627 us (72%)
  other arithmetic  132 us (15%)
  local copies, waits for them, and re-layouts  49.7 us (6%)
  matrix products  48.4 us (6%)
  between operations  14.5 us (2%)
    psum x1, waiting for transfers between devices, on_device(): weight_grad = lax.psum(weight_terms, ('row', 'col')) * factor  269 us
    reduce_scatter x1, waiting for transfers between devices, on_device(): lax.psum_scatter(back_partial.astype(jnp.bfloat16), 'col', scatter_dimens...  125 us
    scatter-add x6, other arithmetic, add_turn(): return summed.at[placed].add(products)  109 us
    reduce_scatter x1, waiting for transfers between devices, on_device(): lax.psum_scatter(partial_value.astype(jnp.bfloat16), 'row', scatter_dimen...  98.7 us
    all_gather x1, waiting for transfers between devices, on_device(): grad_group = lax.all_gather(hidden_grad, 'row', axis=0, tiled=True)  70.5 us
    all_gather x1, waiting for transfers between devices, on_device(): gathered = lax.all_gather(projected, 'col', axis=0, tiled=True)  63.8 us
    dot_general x6, matrix products, add_turn(): jnp.einsum(form, matrix, picked, preferred_element_type=jnp.float32)  41 us
    gather x6, local copies, waits for them, and re-layouts, add_turn(): picked = blocks[wanted]  30.1 us
  transfers between devices with their start and end apart: 5, of which 5 were waited for; matrix products, arithmetic and copies ran while one was open for 1% of the time, Pallas kernels for 0%

commit v1 on v0

v1 whole, which is shorter than its diff:
```python
import jax
import jax.numpy as jnp
from jax import lax
from jax.experimental import pallas as pl
from jax.experimental.pallas import tpu as pltpu
from jax.sharding import PartitionSpec as P

MESH = pl.DeviceIdType.MESH
BF = jnp.bfloat16
F32 = jnp.float32
NZ = 8
NY = 4
BLK = 128
HALF = 512


def remote(src, dst, send, recv, device):
    return pltpu.make_async_remote_copy(
        src_ref=src, dst_ref=dst, send_sem=send, recv_sem=recv,
        device_id=device, device_id_type=MESH,
    )


def kernel(
    slot_of, feat, weight, cot, tiles_in,
    act, fgrad, wgrad,
    xg, proj, hg, tiles, tiles_t, strip, part,
    rr, rrx, rc, rcs, rcr, rcx, dp, dg, ws, wr, wxs, wxr, zg,
    tile_sem,
    a_ys, a_yr, a_xs, a_xr, a_ds, a_dr,
    b_s, b_r, bx_s, bx_r,
    c_s, c_r, cx_s, cx_r,
    e_s, e_r, ex_s, ex_r, ed_s, ed_r,
    t_s, t_r, z_s, z_r, zx_s, zx_r, g_s, g_r,
    w_ys, w_yr, w_xs, w_xr, w_ds, w_dr,
):
    row = lax.axis_index("row")
    col = lax.axis_index("col")
    xl, z = row // NZ, row % NZ
    xh, y, core = col // 8, (col // 2) % NY, col % 2

    def z_dev(k):
        return (xl * NZ + (z + k + NZ) % NZ, col)

    def y_dev(d):
        return (row, xh * 8 + ((y + 1 - 2 * d + NY) % NY) * 2 + core)

    xl_dev = ((1 - xl) * NZ + z, col)
    xh_dev = (row, (1 - xh) * 8 + y * 2 + core)
    sib_dev = (row, xh * 8 + y * 2 + 1 - core)

    load_tiles = pltpu.make_async_copy(tiles_in, tiles.at[pl.ds(0, 64)], tile_sem)
    load_tiles.start()

    barrier = pltpu.get_barrier_semaphore()
    for k in range(1, 16):
        pl.semaphore_signal(barrier, inc=1, device_id=(row, (col + k) % 16), device_id_type=MESH)
    for k in range(1, NZ):
        pl.semaphore_signal(barrier, inc=1, device_id=z_dev(k), device_id_type=MESH)
    pl.semaphore_signal(barrier, inc=1, device_id=xl_dev, device_id_type=MESH)
    pl.semaphore_wait(barrier, 15 + NZ - 1 + 1)

    def gather_col(own, slot, ys, yr, xs, xr, ds, dr):
        def source(d, sub, s, other):
            yy = (y + (2 * d - 1) * s + NY) % NY
            xx = xh if sub == 1 else 1 - xh
            return xx * 8 + yy * 2 + (1 - core if other else core)

        def send_y(d, sub, s):
            here = slot(source(d, sub, s, False), d)
            there = here
            src = own(d) if (sub == 1 and s == 0) else here
            return remote(src, there, ys.at[d, sub, s], yr.at[d, sub, s], y_dev(d))

        def send_d(d, sub, s):
            here = slot(source(d, sub, s, False), d)
            src = own(d) if (sub == 1 and s == 0) else here
            return remote(src, here, ds.at[d, sub, s], dr.at[d, sub, s], sib_dev)

        def send_x(d):
            return remote(own(d), slot(col, d), xs.at[d], xr.at[d], xh_dev)

        def got(d, sub, s):
            here = slot(source(d, sub, s, False), d)
            remote(here, here, ys.at[d, sub, s - 1], yr.at[d, sub, s - 1], y_dev(d)).wait_recv()

        def arrive(sub, s):
            for d in range(2):
                got(d, sub, s)
                if s < NY - 1:
                    send_y(d, sub, s).start()
                send_d(d, sub, s).start()

        def start():
            for d in range(2):
                send_y(d, 1, 0).start()
                send_x(d).start()
                send_d(d, 1, 0).start()

        def go():
            arrive(1, 1)
            for d in range(2):
                here = slot(source(d, 0, 0, False), d)
                remote(here, here, xs.at[d], xr.at[d], xh_dev).wait_recv()
                send_y(d, 0, 0).start()
                send_d(d, 0, 0).start()
            arrive(1, 2)
            arrive(0, 1)
            arrive(1, 3)
            arrive(0, 2)
            arrive(0, 3)
            for sub in (1, 0):
                for s in range(NY):
                    for d in range(2):
                        here = slot(source(d, sub, s, True), d)
                        remote(here, here, ds.at[d, sub, s], dr.at[d, sub, s], sib_dev).wait_recv()

        def drain():
            for d in range(2):
                send_x(d).wait_send()
                for sub in range(2):
                    for s in range(NY):
                        if s < NY - 1:
                            send_y(d, sub, s).wait_send()
                        send_d(d, sub, s).wait_send()

        return start, go, drain

    def feat_half(d):
        return feat.at[pl.ds(64 * d, 64)]

    def xg_slot(c, d):
        return xg.at[pl.ds(pl.multiple_of(c * BLK + 64 * d, 64), 64)]

    fa_start, fa_go, fa_drain = gather_col(feat_half, xg_slot, a_ys, a_yr, a_xs, a_xr, a_ds, a_dr)
    fa_start()
    xg[pl.ds(pl.multiple_of(col * BLK, BLK), BLK), :] = feat[...]
    load_tiles.wait()
    tiles[64] = jnp.zeros((BLK, BLK), BF)
    tiles_t[64] = jnp.zeros((BLK, BLK), BF)

    def flip(t, carry):
        tiles_t[t] = tiles[t].T
        return carry

    lax.fori_loop(0, 64, flip, 0)
    fa_go()

    def project(b, carry):
        rows = pl.ds(pl.multiple_of(b * 256, 256), 256)
        value = jnp.dot(xg[rows, :], weight[...], preferred_element_type=F32).astype(BF)
        proj[0, rows, :] = value[:, :HALF]
        proj[1, rows, :] = value[:, HALF:]
        return carry

    lax.fori_loop(0, 8, project, 0)

    def product(source, table, first, step, base, d):
        for i in range(16):
            strip[:, i * BLK:(i + 1) * BLK] = table[slot_of[first + i * step]]
        return jnp.dot(strip[...], source[d], preferred_element_type=F32)

    def rr_send(q, d, s):
        return remote(rr.at[q, s], rr.at[q, s + 1], b_s.at[q, s], b_r.at[q, s], z_dev(1 - 2 * d))

    def rrx_send(d):
        return remote(rr.at[2 * d, NZ - 1], rrx.at[d], bx_s.at[d], bx_r.at[d], xl_dev)

    def row_step(s, carry):
        def compute(q, inner):
            d, sub = q // 2, q % 2
            zd = (z + (2 * d - 1) * (s + 1) + NZ) % NZ
            xd = xl + (1 - sub) * (1 - 2 * xl)
            part[q] = product(proj, tiles, (xd * NZ + zd) * 16, 1, 0, d)
            return inner

        lax.fori_loop(0, 4, compute, 0)

        def pass_on(q, inner):
            d, sub = q // 2, q % 2

            @pl.when(s > 0)
            def _():
                remote(rr.at[q, s], rr.at[q, s], b_s.at[q, s - 1], b_r.at[q, s - 1],
                       z_dev(1 - 2 * d)).wait_recv()
                part[q] = part[q] + rr[q, s].astype(F32)

            rr[q, s] = part[q].astype(BF)

            @pl.when(s < NZ - 1)
            def _():
                rr_send(q, d, s).start()

            @pl.when((s == NZ - 1) & (sub == 0))
            def _():
                rrx_send(d).start()

            return inner

        lax.fori_loop(0, 4, pass_on, 0)
        return carry

    lax.fori_loop(0, NZ, row_step, 0)

    own_h = pl.ds(pl.multiple_of(row * BLK, BLK), BLK)
    for d in range(2):
        remote(rrx.at[d], rrx.at[d], bx_s.at[d], bx_r.at[d], xl_dev).wait_recv()
        lanes = slice(d * HALF, (d + 1) * HALF)
        hidden = part[2 * d + 1] + rrx[d].astype(F32)
        sig = 1.0 / (1.0 + jnp.exp(-hidden))
        act[:, lanes] = (hidden * sig).astype(BF)
        slope = sig * (1.0 + hidden * (1.0 - sig))
        hg[d, own_h, :] = (cot[:, lanes].astype(F32) * slope).astype(BF)

    def hg_at(d, sub, s):
        zz = (z + (2 * d - 1) * s + NZ) % NZ
        xx = xl if sub == 1 else 1 - xl
        return hg.at[d, pl.ds(pl.multiple_of((xx * NZ + zz) * BLK, BLK), BLK)]

    def ag_send(d, sub, s):
        here = hg_at(d, sub, s)
        return remote(here, here, c_s.at[d, sub, s], c_r.at[d, sub, s], z_dev(1 - 2 * d))

    def agx_send(d):
        here = hg_at(d, 1, 0)
        return remote(here, here, cx_s.at[d], cx_r.at[d], xl_dev)

    def ag_arrive(sub, s):
        for d in range(2):
            here = hg_at(d, sub, s)
            remote(here, here, c_s.at[d, sub, s - 1], c_r.at[d, sub, s - 1],
                   z_dev(1 - 2 * d)).wait_recv()
            if s < NZ - 1:
                ag_send(d, sub, s).start()

    for d in range(2):
        ag_send(d, 1, 0).start()
        agx_send(d).start()
    for d in range(2):
        here = hg_at(d, 0, 0)
        remote(here, here, cx_s.at[d], cx_r.at[d], xl_dev).wait_recv()
        ag_send(d, 0, 0).start()
    for s in range(1, NZ):
        ag_arrive(1, s)
        ag_arrive(0, s)

    def sib_send(q, s):
        return remote(rcs.at[q, s], rcr.at[q, s], ed_s.at[q, s], ed_r.at[q, s], sib_dev)

    def rc_send(q, d, s):
        return remote(rc.at[q, s], rc.at[q, s + 1], e_s.at[q, s], e_r.at[q, s], y_dev(d))

    def rcx_send(d):
        return remote(rc.at[2 * d, NY - 1], rcx.at[d], ex_s.at[d], ex_r.at[d], xh_dev)

    def col_step(s, carry):
        def place(q):
            d, sub = q // 2, q % 2
            yd = (y + (2 * d - 1) * (s + 1) + NY) % NY
            xd = xh + (1 - sub) * (1 - 2 * xh)
            return d, xd * 8 + yd * 2

        def compute_other(q, inner):
            d, base = place(q)
            rcs[q, s] = product(hg, tiles_t, base + 1 - core, 16, 0, d).astype(BF)
            sib_send(q, s).start()
            return inner

        def compute_own(q, inner):
            d, base = place(q)
            part[q] = product(hg, tiles_t, base + core, 16, 0, d)
            return inner

        lax.fori_loop(0, 4, compute_other, 0)
        lax.fori_loop(0, 4, compute_own, 0)

        def pass_on(q, inner):
            d, sub = q // 2, q % 2
            remote(rcr.at[q, s], rcr.at[q, s], ed_s.at[q, s], ed_r.at[q, s], sib_dev).wait_recv()
            part[q] = part[q] + rcr[q, s].astype(F32)

            @pl.when(s > 0)
            def _():
                remote(rc.at[q, s], rc.at[q, s], e_s.at[q, s - 1], e_r.at[q, s - 1],
                       y_dev(d)).wait_recv()
                part[q] = part[q] + rc[q, s].astype(F32)

            rc[q, s] = part[q].astype(BF)

            @pl.when(s < NY - 1)
            def _():
                rc_send(q, d, s).start()

            @pl.when((s == NY - 1) & (sub == 0))
            def _():
                rcx_send(d).start()

            return inner

        lax.fori_loop(0, 4, pass_on, 0)
        return carry

    lax.fori_loop(0, NY, col_step, 0)

    for d in range(2):
        remote(rcx.at[d], rcx.at[d], ex_s.at[d], ex_r.at[d], xh_dev).wait_recv()
        delta = (part[2 * d + 1] + rcx[d].astype(F32)).astype(BF)
        for k in range(4):
            dp[4 * d + k] = delta[:, k * BLK:(k + 1) * BLK]

    def piece_send(k):
        peer = (col + k) % 16
        return remote(dp.at[peer // 2], dg.at[col], t_s.at[k], t_r.at[k], (row, peer))

    for k in range(1, 16):
        piece_send(k).start()
    dg[col] = dp[col // 2]

    delta = jnp.concatenate([dp[k] for k in range(8)], axis=1)
    fgrad[...] = lax.dot_general(
        delta, weight[...], (((1,), (1,)), ((), ())), preferred_element_type=F32
    ).astype(BF)

    for k in range(1, 16):
        there = dg.at[(col - k + 16) % 16]
        remote(there, there, t_s.at[k], t_r.at[k], (row, (col + k) % 16)).wait_recv()
    for i in range(16):
        strip[:, i * BLK:(i + 1) * BLK] = dg[i].T
    lanes = pl.ds(pl.multiple_of(core * HALF, HALF), HALF)
    terms = jnp.dot(strip[...], xg[:, lanes], preferred_element_type=F32).T
    for k in range(NZ):
        ws[k] = terms[k * 64:(k + 1) * 64, :].astype(BF)

    def zsum_send(k):
        return remote(ws.at[(z + k) % NZ], wr.at[z], z_s.at[k], z_r.at[k], z_dev(k))

    for k in range(1, NZ):
        zsum_send(k).start()
    total = ws[z].astype(F32)
    for k in range(1, NZ):
        zz = (z - k + NZ) % NZ
        remote(wr.at[zz], wr.at[zz], z_s.at[k], z_r.at[k], z_dev(k)).wait_recv()
        total = total + wr[zz].astype(F32)
    wxs[...] = total.astype(BF)
    wx_send = remote(wxs, wxr, zx_s, zx_r, xl_dev)
    wx_send.start()
    wx_send.wait_recv()
    zg[pl.ds(pl.multiple_of(z * 64, 64), 64), :] = (wxs[...].astype(F32) + wxr[...].astype(F32)).astype(BF)

    def zg_at(k):
        return zg.at[pl.ds(pl.multiple_of(((z + k + NZ) % NZ) * 64, 64), 64)]

    def zg_send(k):
        return remote(zg_at(0), zg_at(0), g_s.at[k], g_r.at[k], z_dev(k))

    for k in range(1, NZ):
        zg_send(k).start()
    for k in range(1, NZ):
        remote(zg_at(-k), zg_at(-k), g_s.at[k], g_r.at[k], z_dev(k)).wait_recv()

    def zg_half(d):
        return zg.at[pl.ds(256 * d, 256)]

    def wgrad_slot(c, d):
        return wgrad.at[c, pl.ds(256 * d, 256)]

    wa_start, wa_go, wa_drain = gather_col(zg_half, wgrad_slot, w_ys, w_yr, w_xs, w_xr, w_ds, w_dr)
    wa_start()
    wgrad[col] = zg[...]
    wa_go()

    fa_drain()
    wa_drain()
    for d in range(2):
        rrx_send(d).wait_send()
        agx_send(d).wait_send()
        rcx_send(d).wait_send()
        for sub in range(2):
            q = 2 * d + sub
            for s in range(NZ - 1):
                rr_send(q, d, s).wait_send()
                ag_send(d, sub, s).wait_send()
            for s in range(NY - 1):
                rc_send(q, d, s).wait_send()
            for s in range(NY):
                sib_send(q, s).wait_send()
    for k in range(1, 16):
        piece_send(k).wait_send()
    for k in range(1, NZ):
        zsum_send(k).wait_send()
        zg_send(k).wait_send()
    wx_send.wait_send()


def layer(slot_of, features, weight, cotangent, tiles):
    vmem = pl.BlockSpec(memory_space=pltpu.VMEM)
    dma = pltpu.SemaphoreType.DMA
    gather_sems = [dma((2, 2, 3)), dma((2, 2, 3)), dma((2,)), dma((2,)), dma((2, 2, 4)), dma((2, 2, 4))]
    return pl.pallas_call(
        kernel,
        name="layer",
        out_shape=(
            jax.ShapeDtypeStruct((BLK, 1024), BF),
            jax.ShapeDtypeStruct((BLK, 1024), BF),
            jax.ShapeDtypeStruct((16, HALF, BLK), BF),
        ),
        in_specs=[
            pl.BlockSpec(memory_space=pltpu.SMEM), vmem, vmem, vmem,
            pl.BlockSpec(memory_space=pl.ANY),
        ],
        out_specs=(vmem, vmem, vmem),
        scratch_shapes=[
            pltpu.VMEM((2048, 1024), BF),
            pltpu.VMEM((2, 2048, HALF), BF),
            pltpu.VMEM((2, 2048, HALF), BF),
            pltpu.VMEM((65, BLK, BLK), BF),
            pltpu.VMEM((65, BLK, BLK), BF),
            pltpu.VMEM((BLK, 2048), BF),
            pltpu.VMEM((4, BLK, HALF), F32),
            pltpu.VMEM((4, NZ, BLK, HALF), BF),
            pltpu.VMEM((2, BLK, HALF), BF),
            pltpu.VMEM((4, NY, BLK, HALF), BF),
            pltpu.VMEM((4, NY, BLK, HALF), BF),
            pltpu.VMEM((4, NY, BLK, HALF), BF),
            pltpu.VMEM((2, BLK, HALF), BF),
            pltpu.VMEM((8, BLK, BLK), BF),
            pltpu.VMEM((16, BLK, BLK), BF),
            pltpu.VMEM((NZ, 64, BLK), BF),
            pltpu.VMEM((NZ, 64, BLK), BF),
            pltpu.VMEM((64, BLK), BF),
            pltpu.VMEM((64, BLK), BF),
            pltpu.VMEM((HALF, BLK), BF),
            dma,
            *gather_sems,
            dma((4, 7)), dma((4, 7)), dma((2,)), dma((2,)),
            dma((2, 2, 7)), dma((2, 2, 7)), dma((2,)), dma((2,)),
            dma((4, 3)), dma((4, 3)), dma((2,)), dma((2,)), dma((4, 4)), dma((4, 4)),
            dma((16,)), dma((16,)), dma((NZ,)), dma((NZ,)), dma, dma, dma((NZ,)), dma((NZ,)),
            *gather_sems,
        ],
        compiler_params=pltpu.CompilerParams(
            collective_id=0, has_side_effects=True, vmem_limit_bytes=60 * 1024 * 1024,
        ),
    )(slot_of, features, weight, cotangent, tiles)


def on_device(features, weight, cotangent, tile_values, block_row, block_column, tile_count):
    slots = jnp.arange(64, dtype=jnp.int32)
    cell = block_row[0, 0] * 16 + block_column[0, 0]
    cell = jnp.where(slots < tile_count[0, 0], cell, -1)
    named = cell[None, :] == jnp.arange(256, dtype=jnp.int32)[:, None]
    slot_of = jnp.min(jnp.where(named, slots[None, :], 64), axis=1)
    activated, feat_grad, pieces = layer(slot_of, features, weight, cotangent, tile_values[0, 0])
    pieces = pieces.reshape(8, 2, HALF, BLK).transpose(1, 2, 0, 3).reshape(1024, 1024)
    weight_grad = pieces.astype(F32) * 32768 ** (-0.5)
    return activated, feat_grad, weight_grad


def solution(mesh):
    return jax.shard_map(
        on_device,
        mesh=mesh,
        in_specs=(
            P(("row", "col"), None),
            P(),
            P(("col", "row"), None),
            P("row", "col", None, None, None),
            P("row", "col", None),
            P("row", "col", None),
            P("row", "col"),
        ),
        out_specs=(P(("col", "row"), None), P(("row", "col"), None), P()),
        check_vma=False,
    )
```

time: 875 us -> 218 us (0.25)
  waiting for transfers between devices: 627 us -> 0 us
  Pallas kernels: 0 us -> 206 us
  other arithmetic: 132 us -> 3.39 us
  matrix products: 48.4 us -> 0 us
  local copies, waits for them, and re-layouts: 49.7 us -> 6.87 us
  between operations: 14.5 us -> 1.32 us
    psum x1 -> x0, waiting for transfers between devices: 269 us -> none  [on_device(): weight_grad = lax.psum(weight_terms, ('row', 'col')) * factor]
    reduce_scatter x2 -> x0, waiting for transfers between devices: 224 us -> none  [the longest x1 125 us: on_device(): lax.psum_scatter(back_partial.astype(jnp.bfloat16), 'col', scatter_dimens...]
    pallas_call x0 -> x1, Pallas kernels: none -> 206 us  [layer(): pl.pallas_call(kernel, name='layer', out_shape=(jax.ShapeDtypeStruct((BLK...]
    all_gather x2 -> x0, waiting for transfers between devices: 134 us -> none  [the longest x1 70.5 us: on_device(): grad_group = lax.all_gather(hidden_grad, 'row', axis=0, tiled=True)]
    scatter-add x6 -> x0, other arithmetic: 109 us -> none  [add_turn(): return summed.at[placed].add(products)]
    dot_general x9 -> x0, matrix products: 48.4 us -> none  [the longest x6 41 us: add_turn(): jnp.einsum(form, matrix, picked, preferred_element_type=jnp.float32)]
    gather x6 -> x0, local copies, waits for them, and re-layouts: 30.1 us -> none  [add_turn(): picked = blocks[wanted]]
    convert_element_type x9 -> x0, other arithmetic: 18 us -> none  [the longest x1 6.06 us: on_device(): partial_value.astype(jnp.bfloat16)]
  transfers between devices with their start and end apart: 5 -> 0, of which waited for: 5 -> 0; matrix products, arithmetic and copies ran while one was open for 1% -> 0% of each run, Pallas kernels for 0% -> 0%
where the time goes in v1:
time: 218 us
  Pallas kernels  206 us (94%)
  local copies, waits for them, and re-layouts  6.87 us (3%)
  other arithmetic  3.39 us (2%)
    pallas_call x1, Pallas kernels, layer(): pl.pallas_call(kernel, name='layer', out_shape=(jax.ShapeDtypeStruct((BLK...  206 us
    unnamed x7, local copies, waits for them, and re-layouts  4.44 us

profile of v1, /device:TPU:1, one launch (start us, length us, event | category | flops | bytes accessed | tf_op | source)
XLA Modules:
  0.0 218.0 jit_solution(68264966894714661)
XLA Ops:
  1.3 0.7 compare_select_fusion
  2.0 0.7 select_reduce_fusion.slot_of
  2.6 206.4 %layer.1 = (bf16[128,1024]{1,0:T(8,128)(2,1)}, bf16[128,1024]{1,0:T(8,128)(2,1)}, bf16[16,512,128]{2,1,0:T(8,128)(2,1)}) custom-call(s32[256]{0:T(256)} %select_reduce_fusion.slot_of, bf16[128,1024]{1,0:T(8,128)(2,1)} %feat.1, bf16[1024,1024]{1,0:T(8,128)(2,1)} %weight.1, bf16[128,1024]{1,0:T(8,128)(2,1)} %cot.1, bf16[64,128,128]{2,1,0:T(8,128)(2,1)} %bitcast.16), custom_call_target="tpu_custom_call" | custom-call | tf_op jit(solution)/shard_map/layer/pallas_call | solution.py:399
  209.0 2.1 convert_multiply_fusion
  211.1 2.4 %copy.11 = f32[2,512,8,128]{3,2,1,0:T(8,128)S(1)} copy(f32[2,512,8,128]{3,1,0,2:T(8,128)S(1)} %bitcast.13) | data formatting | bytes 8388608 | tf_op jit(solution)/shard_map/mul | solution.py:455
  213.5 0.0 copy-start.1
  213.5 0.0 copy-start
  213.5 3.0 %copy.14 = f32[128,8,8,128]{3,1,2,0:T(8,128)} copy(f32[128,8,8,128]{3,2,1,0:T(8,128)S(1)} %bitcast.14) | data formatting | bytes 8388608
  216.6 0.0 copy-done.1
  216.6 0.7 copy.18
  217.3 0.0 copy-done
  217.3 0.7 copy.19
Async XLA Ops:
  213.5 3.0 %copy-start.1 = (bf16[128,1024]{1,0:T(8,128)(2,1)S(1)}, bf16[128,1024]{1,0:T(8,128)(2,1)}, u32[]{:S(2)}) copy-start(bf16[128,1024]{1,0:T(8,128)(2,1)} %get-tuple-element.12) | copy-start | bytes 786436
  213.5 3.7 %copy-start = (bf16[128,1024]{1,0:T(8,128)(2,1)S(1)}, bf16[128,1024]{1,0:T(8,128)(2,1)}, u32[]{:S(2)}) copy-start(bf16[128,1024]{1,0:T(8,128)(2,1)} %get-tuple-element.13) | copy-start | bytes 786436

commit v2 on v0

v2 whole, which is shorter than its diff:
```python
import jax
import jax.numpy as jnp
from jax import lax
from jax.experimental import pallas as pl
from jax.experimental.pallas import tpu as pltpu
from jax.sharding import PartitionSpec as P

MESH = pl.DeviceIdType.MESH
BF = jnp.bfloat16
F32 = jnp.float32
NZ = 8
NY = 4
BLK = 128
QUART = 256


def remote(src, dst, send, recv, device):
    return pltpu.make_async_remote_copy(
        src_ref=src, dst_ref=dst, send_sem=send, recv_sem=recv,
        device_id=device, device_id_type=MESH,
    )


def kernel(
    slot_of, feat_in, weight_in, cot_in, tiles_in,
    act_out, fgrad_out, wout_out,
    weight, cot, act, fgrad, wout, xg, hg, tiles, tiles_t, strip, part, acc, zq, zt,
    rr, rrx, rb, rbs, rbr, rc, rcs, rcr, rcx,
    vpart, vc, vcs, vcr, vcx, ws, wr, wxs, wxr, wfin,
    load_sem, feat_sem, store_sem,
    a_ys, a_yr, a_xs, a_xr, a_ds, a_dr,
    b_s, b_r, bx_s, bx_r, n_s, n_r, nx_s, nx_r,
    c_s, c_r, cx_s, cx_r,
    e_s, e_r, ex_s, ex_r, ed_s, ed_r,
    v_s, v_r, vx_s, vx_r, vd_s, vd_r,
    z_s, z_r, zx_s, zx_r, k_s, k_r, g_s, g_r, gd_s, gd_r,
):
    row = lax.axis_index("row")
    col = lax.axis_index("col")
    xl, z = row // NZ, row % NZ
    xh, y, core = col // 8, (col // 2) % NY, col % 2
    chip = xh * NY + y

    def z_dev(k):
        return (xl * NZ + (z + k + NZ) % NZ, col)

    def y_dev(d):
        return (row, xh * 8 + ((y + 1 - 2 * d + NY) % NY) * 2 + core)

    xl_dev = ((1 - xl) * NZ + z, col)
    xh_dev = (row, (1 - xh) * 8 + y * 2 + core)
    sib_dev = (row, xh * 8 + y * 2 + 1 - core)

    def chip_dev(k):
        other = (chip + k) % 8
        return (row, other * 2 + core)

    def feat_load(p, d):
        lanes = pl.ds((2 * p + d) * QUART, QUART)
        return pltpu.make_async_copy(
            feat_in.at[:, lanes], xg.at[p, d, pl.ds(pl.multiple_of(col * BLK, BLK), BLK)], feat_sem.at[p, d])

    loads = [
        pltpu.make_async_copy(tiles_in, tiles.at[pl.ds(0, 64)], load_sem.at[0]),
        pltpu.make_async_copy(weight_in, weight, load_sem.at[1]),
        pltpu.make_async_copy(cot_in, cot, load_sem.at[2]),
    ]
    barrier = pltpu.get_barrier_semaphore()
    peers = [chip_dev(k) for k in range(1, 8)] + [z_dev(k) for k in range(1, NZ)] + [xl_dev, sib_dev]
    for peer in peers:
        pl.semaphore_signal(barrier, inc=1, device_id=peer, device_id_type=MESH)
    for p in range(2):
        for d in range(2):
            feat_load(p, d).start()
    for load in loads:
        load.start()
    for p in range(2):
        for d in range(2):
            feat_load(p, d).wait()
    pl.semaphore_wait(barrier, len(peers))

    def col_source(d, sub, s, other):
        yy = (y + (2 * d - 1) * s + NY) % NY
        xx = xh if sub == 1 else 1 - xh
        return xx * 8 + yy * 2 + (1 - core if other else core)

    def xg_at(p, d, c):
        return xg.at[p, d, pl.ds(pl.multiple_of(c * BLK, BLK), BLK)]

    def ac_send(p, d, sub, s, to_y):
        here = xg_at(p, d, col_source(d, sub, s, False))
        if to_y:
            remote(here, here, a_ys.at[p, d, sub], a_yr.at[p, d, sub, s], y_dev(d)).start()
        else:
            remote(here, here, a_ds.at[p, d, sub], a_dr.at[p, d, sub, s], sib_dev).start()

    def ac_start(p):
        for d in range(2):
            ac_send(p, d, 1, 0, True)
            remote(xg_at(p, d, col), xg_at(p, d, col), a_xs.at[p, d], a_xr.at[p, d], xh_dev).start()
        for d in range(2):
            ac_send(p, d, 1, 0, False)

    def ac_event(p, e):
        sub, s = ((1, 1), (0, 0), (1, 2), (0, 1), (1, 3), (0, 2), (0, 3))[e]
        for d in range(2):
            here = xg_at(p, d, col_source(d, sub, s, False))
            if s == 0:
                remote(here, here, a_xs.at[p, d], a_xr.at[p, d], xh_dev).wait_recv()
            else:
                remote(here, here, a_ys.at[p, d, sub], a_yr.at[p, d, sub, s - 1], y_dev(d)).wait_recv()
            if s < NY - 1:
                ac_send(p, d, sub, s, True)
            ac_send(p, d, sub, s, False)

    def ac_finish(p):
        for sub in (1, 0):
            for s in range(NY):
                for d in range(2):
                    here = xg_at(p, d, col_source(d, sub, s, True))
                    remote(here, here, a_ds.at[p, d, sub], a_dr.at[p, d, sub, s], sib_dev).wait_recv()

    def product(source, table, first, step):
        for i in range(16):
            strip[:, i * BLK:(i + 1) * BLK] = table[slot_of[first + i * step]]
        return jnp.dot(strip[...], source, preferred_element_type=F32)

    def z_dest(d, s):
        return (z + (2 * d - 1) * (s + 1) + NZ) % NZ

    def row_step(s):
        def compute(q, inner):
            d, sub = q // 2, q % 2
            xd = xl + (1 - sub) * (1 - 2 * xl)
            part[0, q] = product(xg[0, d], tiles, (xd * NZ + z_dest(d, s)) * 16, 1)
            return inner

        def pass_on(q, inner):
            d, sub = q // 2, q % 2
            if s > 0:
                here = rr.at[q, s]
                remote(here, here, b_s.at[q], b_r.at[q, s - 1], z_dev(1 - 2 * d)).wait_recv()
                part[0, q] = part[0, q] + rr[q, s].astype(F32)
            rr[q, s] = part[0, q].astype(BF)
            if s < NZ - 1:
                remote(rr.at[q, s], rr.at[q, s + 1], b_s.at[q], b_r.at[q, s], z_dev(1 - 2 * d)).start()
            else:
                @pl.when(sub == 0)
                def _():
                    remote(rr.at[q, s], rrx.at[d], bx_s.at[d], bx_r.at[d], xl_dev).start()
            return inner

        lax.fori_loop(0, 4, compute, 0)
        lax.fori_loop(0, 4, pass_on, 0)

    def row_other(s):
        def one(d, inner):
            rbs[d, s] = product(xg[1, d], tiles, ((1 - xl) * NZ + z_dest(d, s)) * 16, 1).astype(BF)
            remote(rbs.at[d, s], rbr.at[d, s], nx_s.at[d], nx_r.at[d, s], xl_dev).start()
            return inner

        lax.fori_loop(0, 2, one, 0)

    def row_own(s):
        def one(d, inner):
            part[1, d] = product(xg[1, d], tiles, (xl * NZ + z_dest(d, s)) * 16, 1)
            return inner

        lax.fori_loop(0, 2, one, 0)

    def row_pass(s):
        def one(d, inner):
            here = rbr.at[d, s]
            remote(here, here, nx_s.at[d], nx_r.at[d, s], xl_dev).wait_recv()
            part[1, d] = part[1, d] + rbr[d, s].astype(F32)
            if s > 0:
                here = rb.at[d, s]
                remote(here, here, n_s.at[d], n_r.at[d, s - 1], z_dev(1 - 2 * d)).wait_recv()
                part[1, d] = part[1, d] + rb[d, s].astype(F32)
            if s < NZ - 1:
                rb[d, s] = part[1, d].astype(BF)
                remote(rb.at[d, s], rb.at[d, s + 1], n_s.at[d], n_r.at[d, s], z_dev(1 - 2 * d)).start()
            return inner

        lax.fori_loop(0, 2, one, 0)

    def row_finish(p):
        for d in range(2):
            if p == 0:
                remote(rrx.at[d], rrx.at[d], bx_s.at[d], bx_r.at[d], xl_dev).wait_recv()
                zq[d] = (part[0, 2 * d + 1] + rrx[d].astype(F32)).astype(BF)
            else:
                zq[2 + d] = part[1, d].astype(BF)
        both = jnp.concatenate([zq[2 * p], zq[2 * p + 1]], axis=1)
        value = jnp.dot(both, weight[pl.ds(p * 512, 512), :], preferred_element_type=F32)
        if p == 0:
            acc[...] = value
        else:
            acc[...] = acc[...] + value

    own_h = pl.ds(pl.multiple_of(row * BLK, BLK), BLK)

    def activate(p):
        for d in range(2):
            lanes = slice((2 * p + d) * QUART, (2 * p + d + 1) * QUART)
            hidden = acc[:, lanes]
            sig = 1.0 / (1.0 + jnp.exp(-hidden))
            act[:, lanes] = (hidden * sig).astype(BF)
            slope = sig * (1.0 + hidden * (1.0 - sig))
            hg[p, d, own_h, :] = (cot[:, lanes].astype(F32) * slope).astype(BF)

    def hg_at(p, d, sub, s):
        zz = (z + (2 * d - 1) * s + NZ) % NZ
        xx = xl if sub == 1 else 1 - xl
        return hg.at[p, d, pl.ds(pl.multiple_of((xx * NZ + zz) * BLK, BLK), BLK)]

    def ag_send(p, d, sub, s):
        here = hg_at(p, d, sub, s)
        remote(here, here, c_s.at[p, d, sub], c_r.at[p, d, sub, s], z_dev(1 - 2 * d)).start()

    def ag_cross(p, d, s):
        here = hg_at(p, d, 1, s)
        remote(here, here, cx_s.at[p, d], cx_r.at[p, d, s], xl_dev).start()

    def ag_start(p):
        for d in range(2):
            ag_send(p, d, 1, 0)
            ag_cross(p, d, 0)

    def ag_partner(p, s):
        for d in range(2):
            here = hg_at(p, d, 0, s)
            remote(here, here, cx_s.at[p, d], cx_r.at[p, d, s], xl_dev).wait_recv()
            if p == 0:
                ag_send(p, d, 0, 0)

    def ag_step(p, sub, s):
        for d in range(2):
            here = hg_at(p, d, sub, s)
            remote(here, here, c_s.at[p, d, sub], c_r.at[p, d, sub, s - 1], z_dev(1 - 2 * d)).wait_recv()
            if s < NZ - 1:
                ag_send(p, d, sub, s)
            if p == 1:
                ag_cross(p, d, s)

    def col_place(q, s):
        d, sub = q // 2, q % 2
        yd = (y + (2 * d - 1) * (s + 1) + NY) % NY
        xd = xh + (1 - sub) * (1 - 2 * xh)
        return d, sub, xd * NY + yd

    def col_compute(p, s):
        def other(q, inner):
            d, _, there = col_place(q, s)
            rcs[p, q, s] = product(hg[p, d], tiles_t, there * 2 + 1 - core, 16).astype(BF)
            remote(rcs.at[p, q, s], rcr.at[p, q, s], ed_s.at[p, q], ed_r.at[p, q, s], sib_dev).start()
            return inner

        def own(q, inner):
            d, _, there = col_place(q, s)
            part[p, q] = product(hg[p, d], tiles_t, there * 2 + core, 16)
            return inner

        lax.fori_loop(0, 4, other, 0)
        lax.fori_loop(0, 4, own, 0)

    def col_pass(p, s):
        def pass_on(q, inner):
            d, sub = q // 2, q % 2
            here = rcr.at[p, q, s]
            remote(here, here, ed_s.at[p, q], ed_r.at[p, q, s], sib_dev).wait_recv()
            part[p, q] = part[p, q] + rcr[p, q, s].astype(F32)
            if s > 0:
                here = rc.at[p, q, s]
                remote(here, here, e_s.at[p, q], e_r.at[p, q, s - 1], y_dev(d)).wait_recv()
                part[p, q] = part[p, q] + rc[p, q, s].astype(F32)
            rc[p, q, s] = part[p, q].astype(BF)
            if s < NY - 1:
                remote(rc.at[p, q, s], rc.at[p, q, s + 1], e_s.at[p, q], e_r.at[p, q, s], y_dev(d)).start()
            else:
                @pl.when(sub == 0)
                def _():
                    remote(rc.at[p, q, s], rcx.at[p, d], ex_s.at[p, d], ex_r.at[p, d], xh_dev).start()
            return inner

        lax.fori_loop(0, 4, pass_on, 0)

    def col_finish(p):
        delta = []
        for d in range(2):
            remote(rcx.at[p, d], rcx.at[p, d], ex_s.at[p, d], ex_r.at[p, d], xh_dev).wait_recv()
            delta.append((part[p, 2 * d + 1] + rcx[p, d].astype(F32)).astype(BF))
        value = lax.dot_general(
            jnp.concatenate(delta, axis=1), weight[:, pl.ds(p * 512, 512)],
            (((1,), (1,)), ((), ())), preferred_element_type=F32,
        )
        if p == 0:
            acc[...] = value
        else:
            fgrad[...] = (acc[...] + value).astype(BF)

    def turn_z():
        for k in range(8):
            zt[k] = zq[k // 2, :, (k % 2) * BLK:(k % 2 + 1) * BLK].T

    def wt_compute(s):
        def both(q, inner):
            d, _, there = col_place(q, s)
            tile = zt[there]
            vcs[q, s] = jnp.dot(tile, hg[1 - core, d, own_h, :], preferred_element_type=F32).astype(BF)
            remote(vcs.at[q, s], vcr.at[q, s], vd_s.at[q], vd_r.at[q, s], sib_dev).start()
            vpart[q] = jnp.dot(tile, hg[core, d, own_h, :], preferred_element_type=F32)
            return inner

        lax.fori_loop(0, 4, both, 0)

    def wt_pass(s):
        def pass_on(q, inner):
            d, sub = q // 2, q % 2
            here = vcr.at[q, s]
            remote(here, here, vd_s.at[q], vd_r.at[q, s], sib_dev).wait_recv()
            vpart[q] = vpart[q] + vcr[q, s].astype(F32)
            if s > 0:
                here = vc.at[q, s]
                remote(here, here, v_s.at[q], v_r.at[q, s - 1], y_dev(d)).wait_recv()
                vpart[q] = vpart[q] + vc[q, s].astype(F32)
            vc[q, s] = vpart[q].astype(BF)
            if s < NY - 1:
                remote(vc.at[q, s], vc.at[q, s + 1], v_s.at[q], v_r.at[q, s], y_dev(d)).start()
            else:
                @pl.when(sub == 0)
                def _():
                    remote(vc.at[q, s], vcx.at[d], vx_s.at[d], vx_r.at[d], xh_dev).start()
            return inner

        lax.fori_loop(0, 4, pass_on, 0)

    def wt_spread():
        for d in range(2):
            remote(vcx.at[d], vcx.at[d], vx_s.at[d], vx_r.at[d], xh_dev).wait_recv()
            value = (vpart[2 * d + 1] + vcx[d].astype(F32)).astype(BF)
            for k in range(NZ):
                ws[k, :, d * QUART:(d + 1) * QUART] = value[16 * k:16 * (k + 1), :]
        for k in range(1, NZ):
            remote(ws.at[(z + k) % NZ], wr.at[z], z_s, z_r.at[k], z_dev(k)).start()

    def wt_sum():
        total = ws[z].astype(F32)
        for k in range(1, NZ):
            zz = (z - k + NZ) % NZ
            remote(wr.at[zz], wr.at[zz], z_s, z_r.at[k], z_dev(k)).wait_recv()
            total = total + wr[zz].astype(F32)
        wxs[...] = total.astype(BF)
        remote(wxs, wxr, zx_s, zx_r, xl_dev).start()

    def wout_at(k, zz, side):
        lanes = pl.ds(pl.multiple_of(side * 512, 512), 512)
        return wout.at[k, zz, :, lanes]

    def wt_share():
        remote(wxr, wxr, zx_s, zx_r, xl_dev).wait_recv()
        value = (wxs[...].astype(F32) + wxr[...].astype(F32)).astype(BF)
        wfin[...] = value
        wout[chip, z, :, pl.ds(pl.multiple_of(core * 512, 512), 512)] = value
        for k in range(1, 8):
            remote(wfin, wout_at(chip, z, core), k_s, k_r.at[k], chip_dev(k)).start()

    def wz_at(k, side):
        lanes = pl.ds(pl.multiple_of(side * 512, 512), 512)
        return wout.at[:, (z + k + NZ) % NZ, :, lanes]

    def wz_send(d, s):
        here = wz_at((2 * d - 1) * s, core)
        if s < (NZ // 2 if d == 0 else NZ // 2 - 1):
            remote(here, here, g_s.at[d], g_r.at[d, s], z_dev(1 - 2 * d)).start()
        if s > 0 or d == 0:
            remote(here, here, gd_s, gd_r.at[d, s], sib_dev).start()

    def wz_start():
        for k in range(1, 8):
            there = wout_at((chip - k + 8) % 8, z, core)
            remote(there, there, k_s, k_r.at[k], chip_dev(k)).wait_recv()
        for d in range(2):
            wz_send(d, 0)

    def wz_step(s):
        for d in range(2):
            if s <= (NZ // 2 if d == 0 else NZ // 2 - 1):
                here = wz_at((2 * d - 1) * s, core)
                remote(here, here, g_s.at[d], g_r.at[d, s - 1], z_dev(1 - 2 * d)).wait_recv()
                wz_send(d, s)

    def wz_finish():
        for d in range(2):
            for s in range(NZ // 2 + 1 if d == 0 else NZ // 2):
                if s > 0 or d == 0:
                    here = wz_at((2 * d - 1) * s, 1 - core)
                    remote(here, here, gd_s, gd_r.at[d, s], sib_dev).wait_recv()

    def flip(lo, n):
        def one(t, carry):
            tiles_t[t] = tiles[t].T
            return carry
        lax.fori_loop(lo, lo + n, one, 0)

    ac_start(0)
    ac_start(1)
    loads[0].wait()
    tiles[64] = jnp.zeros((BLK, BLK), BF)
    tiles_t[64] = jnp.zeros((BLK, BLK), BF)
    ac_event(0, 0)
    for e in range(6):
        ac_event(0, e + 1)
        ac_event(1, e)
    ac_finish(0)
    row_step(0)
    ac_event(1, 6)
    ac_finish(1)
    loads[1].wait()
    loads[2].wait()
    row_other(0)
    row_own(0)
    for s in range(NZ):
        if s < NZ - 1:
            row_step(s + 1)
            row_other(s + 1)
        row_pass(s)
        if s < NZ - 1:
            row_own(s + 1)
        flip(8 * s, 8)
    row_finish(0)
    row_finish(1)
    activate(0)
    ag_start(0)
    activate(1)
    act_store = pltpu.make_async_copy(act, act_out, store_sem.at[0])
    act_store.start()
    ag_start(1)
    ag_partner(0, 0)
    turn_z()
    wt_compute(0)
    for s in range(1, NZ):
        ag_step(0, 1, s)
        ag_step(1, 1, s)
        ag_step(0, 0, s)
        if s == 2:
            wt_pass(0)
            wt_compute(1)
        if s == 3:
            wt_pass(1)
            wt_compute(2)
        if s == 5:
            wt_pass(2)
            wt_compute(3)
        if s == 6:
            wt_pass(3)
        if s == 7:
            wt_spread()
    col_compute(0, 0)
    for s in range(NZ):
        ag_partner(1, s)
    col_compute(1, 0)
    wt_sum()
    col_pass(0, 0)
    col_compute(0, 1)
    col_pass(1, 0)
    wt_share()
    col_compute(1, 1)
    col_pass(0, 1)
    col_compute(0, 2)
    wz_start()
    col_pass(1, 1)
    col_compute(1, 2)
    col_pass(0, 2)
    col_compute(0, 3)
    wz_step(1)
    col_pass(1, 2)
    col_compute(1, 3)
    wz_step(2)
    col_pass(0, 3)
    wz_step(3)
    col_pass(1, 3)
    col_finish(0)
    wz_step(4)
    col_finish(1)
    fgrad_store = pltpu.make_async_copy(fgrad, fgrad_out, store_sem.at[1])
    fgrad_store.start()
    wz_finish()
    wout_store = pltpu.make_async_copy(wout, wout_out, store_sem.at[2])
    wout_store.start()
    fgrad_store.wait()
    wout_store.wait()
    act_store.wait()

    for p in range(2):
        for d in range(2):
            for sub in range(2):
                q = 2 * d + sub
                sent = xg.at[p, d, pl.ds(0, 3 * BLK)]
                remote(sent, sent, a_ys.at[p, d, sub], a_yr.at[p, d, sub, 0], y_dev(d)).wait_send()
                sent = xg.at[p, d, pl.ds(0, 4 * BLK)]
                remote(sent, sent, a_ds.at[p, d, sub], a_dr.at[p, d, sub, 0], sib_dev).wait_send()
                if (p == 0 or sub == 1):
                    sent = hg.at[p, d, pl.ds(0, 7 * BLK)]
                    remote(sent, sent, c_s.at[p, d, sub], c_r.at[p, d, sub, 0], z_dev(1)).wait_send()
                sent = rc.at[p, q, pl.ds(0, NY - 1)]
                remote(sent, sent, e_s.at[p, q], e_r.at[p, q, 0], y_dev(d)).wait_send()
                remote(rcs.at[p, q], rcs.at[p, q], ed_s.at[p, q], ed_r.at[p, q, 0], sib_dev).wait_send()
            remote(xg_at(p, d, col), xg_at(p, d, col), a_xs.at[p, d], a_xr.at[p, d], xh_dev).wait_send()
            sent = hg.at[p, d, pl.ds(0, (8 if p else 1) * BLK)]
            remote(sent, sent, cx_s.at[p, d], cx_r.at[p, d, 0], xl_dev).wait_send()
            remote(rcx.at[p, d], rcx.at[p, d], ex_s.at[p, d], ex_r.at[p, d], xh_dev).wait_send()
    for q in range(4):
        sent = rr.at[q, pl.ds(0, NZ - 1)]
        remote(sent, sent, b_s.at[q], b_r.at[q, 0], z_dev(1)).wait_send()
    for d in range(2):
        sent = rb.at[d, pl.ds(0, NZ - 1)]
        remote(sent, sent, n_s.at[d], n_r.at[d, 0], z_dev(1)).wait_send()
        remote(rbs.at[d], rbs.at[d], nx_s.at[d], nx_r.at[d, 0], xl_dev).wait_send()
        remote(rrx.at[d], rrx.at[d], bx_s.at[d], bx_r.at[d], xl_dev).wait_send()
    for q in range(4):
        sent = vc.at[q, pl.ds(0, NY - 1)]
        remote(sent, sent, v_s.at[q], v_r.at[q, 0], y_dev(0)).wait_send()
        remote(vcs.at[q], vcs.at[q], vd_s.at[q], vd_r.at[q, 0], sib_dev).wait_send()
    for d in range(2):
        remote(vcx.at[d], vcx.at[d], vx_s.at[d], vx_r.at[d], xh_dev).wait_send()
    sent = wr.at[pl.ds(0, 7)]
    remote(sent, sent, z_s, z_r.at[1], z_dev(1)).wait_send()
    sent = wr.at[pl.ds(0, 7)]
    remote(sent, sent, k_s, k_r.at[1], chip_dev(1)).wait_send()
    remote(wxs, wxs, zx_s, zx_r, xl_dev).wait_send()
    for d in range(2):
        sent = wout.at[:, pl.ds(0, NZ // 2 - d), :, pl.ds(0, 512)]
        remote(sent, sent, g_s.at[d], g_r.at[d, 0], z_dev(1)).wait_send()
    sent = wout.at[:, :, :, pl.ds(0, 512)]
    remote(sent, sent, gd_s, gd_r.at[0, 0], sib_dev).wait_send()


def layer(slot_of, features, weight, cotangent, tiles):
    hbm = pl.BlockSpec(memory_space=pl.ANY)
    dma = pltpu.SemaphoreType.DMA
    chunk = (BLK, QUART)
    return pl.pallas_call(
        kernel,
        name="layer",
        out_shape=(
            jax.ShapeDtypeStruct((BLK, 1024), BF),
            jax.ShapeDtypeStruct((BLK, 1024), BF),
            jax.ShapeDtypeStruct((8, NZ, 16, 1024), BF),
        ),
        in_specs=[pl.BlockSpec(memory_space=pltpu.SMEM)] + [hbm] * 4,
        out_specs=(hbm, hbm, hbm),
        scratch_shapes=[
            pltpu.VMEM((1024, 1024), BF),
            pltpu.VMEM((BLK, 1024), BF),
            pltpu.VMEM((BLK, 1024), BF),
            pltpu.VMEM((BLK, 1024), BF),
            pltpu.VMEM((8, NZ, 16, 1024), BF),
            pltpu.VMEM((2, 2, 2048, QUART), BF),
            pltpu.VMEM((2, 2, 2048, QUART), BF),
            pltpu.VMEM((65, BLK, BLK), BF),
            pltpu.VMEM((65, BLK, BLK), BF),
            pltpu.VMEM((BLK, 2048), BF),
            pltpu.VMEM((2, 4, *chunk), F32),
            pltpu.VMEM((BLK, 1024), F32),
            pltpu.VMEM((4, *chunk), BF),
            pltpu.VMEM((8, BLK, BLK), BF),
            pltpu.VMEM((4, NZ, *chunk), BF),
            pltpu.VMEM((2, *chunk), BF),
            pltpu.VMEM((2, NZ, *chunk), BF),
            pltpu.VMEM((2, NZ, *chunk), BF),
            pltpu.VMEM((2, NZ, *chunk), BF),
            pltpu.VMEM((2, 4, NY, *chunk), BF),
            pltpu.VMEM((2, 4, NY, *chunk), BF),
            pltpu.VMEM((2, 4, NY, *chunk), BF),
            pltpu.VMEM((2, 2, *chunk), BF),
            pltpu.VMEM((4, *chunk), F32),
            pltpu.VMEM((4, NY, *chunk), BF),
            pltpu.VMEM((4, NY, *chunk), BF),
            pltpu.VMEM((4, NY, *chunk), BF),
            pltpu.VMEM((2, *chunk), BF),
            pltpu.VMEM((NZ, 16, 512), BF),
            pltpu.VMEM((NZ, 16, 512), BF),
            pltpu.VMEM((16, 512), BF),
            pltpu.VMEM((16, 512), BF),
            pltpu.VMEM((16, 512), BF),
            dma((3,)), dma((2, 2)), dma((3,)),
            dma((2, 2, 2)), dma((2, 2, 2, 3)), dma((2, 2)), dma((2, 2)), dma((2, 2, 2)), dma((2, 2, 2, 4)),
            dma((4,)), dma((4, 7)), dma((2,)), dma((2,)), dma((2,)), dma((2, 7)), dma((2,)), dma((2, 8)),
            dma((2, 2, 2)), dma((2, 2, 2, 7)), dma((2, 2)), dma((2, 2, 8)),
            dma((2, 4)), dma((2, 4, 3)), dma((2, 2)), dma((2, 2)), dma((2, 4)), dma((2, 4, 4)),
            dma((4,)), dma((4, 3)), dma((2,)), dma((2,)), dma((4,)), dma((4, 4)),
            dma, dma((NZ,)), dma, dma, dma, dma((NZ,)), dma((2,)), dma((2, 4)), dma, dma((2, 5)),
        ],
        compiler_params=pltpu.CompilerParams(
            collective_id=0, has_side_effects=True, vmem_limit_bytes=60 * 1024 * 1024,
        ),
    )(slot_of, features, weight, cotangent, tiles)


def on_device(features, weight, cotangent, tile_values, block_row, block_column, tile_count):
    slots = jnp.arange(64, dtype=jnp.int32)
    cell = block_row[0, 0] * 16 + block_column[0, 0]
    cell = jnp.where(slots < tile_count[0, 0], cell, -1)
    named = cell[None, :] == jnp.arange(256, dtype=jnp.int32)[:, None]
    slot_of = jnp.min(jnp.where(named, slots[None, :], 64), axis=1)
    activated, feat_grad, pieces = layer(slot_of, features, weight, cotangent, tile_values[0, 0])
    weight_grad = pieces.reshape(1024, 1024).astype(F32) * 32768 ** (-0.5)
    return activated, feat_grad, weight_grad


def solution(mesh):
    return jax.shard_map(
        on_device,
        mesh=mesh,
        in_specs=(
            P(("row", "col"), None),
            P(),
            P(("col", "row"), None),
            P("row", "col", None, None, None),
            P("row", "col", None),
            P("row", "col", None),
            P("row", "col"),
        ),
        out_specs=(P(("col", "row"), None), P(("row", "col"), None), P()),
        check_vma=False,
    )
```

time: 875 us -> 162 us (0.19)
  waiting for transfers between devices: 627 us -> 0 us
  Pallas kernels: 0 us -> 153 us
  other arithmetic: 132 us -> 5.65 us
  matrix products: 48.4 us -> 0 us
  local copies, waits for them, and re-layouts: 49.7 us -> 1.41 us
  between operations: 14.5 us -> 1.3 us
    psum x1 -> x0, waiting for transfers between devices: 269 us -> none  [on_device(): weight_grad = lax.psum(weight_terms, ('row', 'col')) * factor]
    reduce_scatter x2 -> x0, waiting for transfers between devices: 224 us -> none  [the longest x1 125 us: on_device(): lax.psum_scatter(back_partial.astype(jnp.bfloat16), 'col', scatter_dimens...]
    pallas_call x0 -> x1, Pallas kernels: none -> 153 us  [layer(): pl.pallas_call(kernel, name='layer', out_shape=(jax.ShapeDtypeStruct((BLK...]
    all_gather x2 -> x0, waiting for transfers between devices: 134 us -> none  [the longest x1 70.5 us: on_device(): grad_group = lax.all_gather(hidden_grad, 'row', axis=0, tiled=True)]
    scatter-add x6 -> x0, other arithmetic: 109 us -> none  [add_turn(): return summed.at[placed].add(products)]
    dot_general x9 -> x0, matrix products: 48.4 us -> none  [the longest x6 41 us: add_turn(): jnp.einsum(form, matrix, picked, preferred_element_type=jnp.float32)]
    gather x6 -> x0, local copies, waits for them, and re-layouts: 30.1 us -> none  [add_turn(): picked = blocks[wanted]]
    convert_element_type x9 -> x0, other arithmetic: 18 us -> none  [the longest x1 6.06 us: on_device(): partial_value.astype(jnp.bfloat16)]
  transfers between devices with their start and end apart: 5 -> 0, of which waited for: 5 -> 0; matrix products, arithmetic and copies ran while one was open for 1% -> 0% of each run, Pallas kernels for 0% -> 0%
where the time goes in v2:
time: 162 us
  Pallas kernels  153 us (94%)
  other arithmetic  5.65 us (3%)
    pallas_call x1, Pallas kernels, layer(): pl.pallas_call(kernel, name='layer', out_shape=(jax.ShapeDtypeStruct((BLK...  153 us
    mul x1, other arithmetic, on_device(): weight_grad = pieces.reshape(1024, 1024).astype(F32) * 32768 ** (-0.5)  4.32 us

profile of v2, /device:TPU:1, one launch (start us, length us, event | category | flops | bytes accessed | tf_op | source)
XLA Modules:
  0.0 161.8 jit_solution(6272933582148460862)
XLA Ops:
  1.3 0.7 compare_select_fusion
  2.0 0.7 select_reduce_fusion.slot_of
  2.6 153.5 %layer.1 = (bf16[128,1024]{1,0:T(8,128)(2,1)}, bf16[128,1024]{1,0:T(8,128)(2,1)}, bf16[8,8,16,1024]{3,2,1,0:T(8,128)(2,1)}) custom-call(s32[256]{0:T(256)} %select_reduce_fusion.slot_of, bf16[128,1024]{1,0:T(8,128)(2,1)} %feat_in.1, bf16[1024,1024]{1,0:T(8,128)(2,1)} %weight_in.1, bf16[128,1024]{1,0:T(8,128)(2,1)} %cot_in.1, bf16[64,128,128]{2,1,0:T(8,128)(2,1)} %bitcast.7), custom_call_target="tpu_custom_call" | custom-call | tf_op jit(solution)/shard_map/layer/pallas_call | solution.py:543
  156.1 0.0 copy-start.1
  156.1 0.0 copy-start
  156.1 4.3 %convert_multiply_fusion = f32[8,8,16,1024]{3,2,1,0:T(8,128)} fusion(bf16[8,8,16,1024]{3,2,1,0:T(8,128)(2,1)} %get-tuple-element.8), kind=kLoop, calls=%fused_computation | loop fusion | flops 2097152 | bytes 6291456 | tf_op jit(solution)/shard_map/mul | solution.py:608
  160.4 0.0 copy-done.1
  160.4 0.7 copy.13
  161.1 0.0 copy-done
  161.1 0.7 copy.14
Async XLA Ops:
  156.1 4.3 %copy-start.1 = (bf16[128,1024]{1,0:T(8,128)(2,1)S(1)}, bf16[128,1024]{1,0:T(8,128)(2,1)}, u32[]{:S(2)}) copy-start(bf16[128,1024]{1,0:T(8,128)(2,1)} %get-tuple-element.12) | copy-start | bytes 786436
  156.1 5.0 %copy-start = (bf16[128,1024]{1,0:T(8,128)(2,1)S(1)}, bf16[128,1024]{1,0:T(8,128)(2,1)}, u32[]{:S(2)}) copy-start(bf16[128,1024]{1,0:T(8,128)(2,1)} %get-tuple-element.13) | copy-start | bytes 786436

commit v3 on v2

v3 whole, which is shorter than its diff:
```python
import jax
import jax.numpy as jnp
from jax import lax
from jax.experimental import pallas as pl
from jax.experimental.pallas import tpu as pltpu
from jax.sharding import PartitionSpec as P

MESH = pl.DeviceIdType.MESH
BF = jnp.bfloat16
F32 = jnp.float32
NZ = 8
NY = 4
BLK = 128
QUART = 256


def remote(src, dst, send, recv, device):
    return pltpu.make_async_remote_copy(
        src_ref=src, dst_ref=dst, send_sem=send, recv_sem=recv,
        device_id=device, device_id_type=MESH,
    )


def kernel(
    slot_of, feat_in, weight_in, cot_in, tiles_in,
    act_out, fgrad_out, wout_out,
    weight, cot, act, fgrad, wout, xg, hg, tiles, tiles_t, strip, acc, zq, zt,
    part, fin, rr, rrs, rrx, rb, rbs, rbr, rc, rcs, rcr, rcf, rcx,
    vpart, vfin, vc, vcs, vcr, vcf, vcx, ws, wr, wxs, wxr, wfin,
    load_sem, feat_sem, store_sem,
    a_ys, a_yr, a_xs, a_xr, a_ds, a_dr,
    b_s, b_r, bx_s, bx_r, n_s, n_r, nx_s, nx_r,
    c_s, c_r, cx_s, cx_r,
    e_s, e_r, ex_s, ex_r, ed_s, ed_r,
    v_s, v_r, vx_s, vx_r, vd_s, vd_r,
    z_s, z_r, zx_s, zx_r, k_s, k_r, g_s, g_r, gd_s, gd_r,
):
    row = lax.axis_index("row")
    col = lax.axis_index("col")
    xl, z = row // NZ, row % NZ
    xh, y, core = col // 8, (col // 2) % NY, col % 2
    chip = xh * NY + y

    def z_dev(k):
        return (xl * NZ + (z + k + NZ) % NZ, col)

    def y_dev(d):
        return (row, xh * 8 + ((y + 1 - 2 * d + NY) % NY) * 2 + core)

    xl_dev = ((1 - xl) * NZ + z, col)
    xh_dev = (row, (1 - xh) * 8 + y * 2 + core)
    sib_dev = (row, xh * 8 + y * 2 + 1 - core)

    def chip_dev(k):
        other = (chip + k) % 8
        return (row, other * 2 + core)

    def feat_load(p, d):
        lanes = pl.ds((2 * p + d) * QUART, QUART)
        return pltpu.make_async_copy(
            feat_in.at[:, lanes], xg.at[p, d, pl.ds(pl.multiple_of(col * BLK, BLK), BLK)], feat_sem.at[p, d])

    loads = [
        pltpu.make_async_copy(tiles_in, tiles.at[pl.ds(0, 64)], load_sem.at[0]),
        pltpu.make_async_copy(weight_in, weight, load_sem.at[1]),
        pltpu.make_async_copy(cot_in, cot, load_sem.at[2]),
    ]
    barrier = pltpu.get_barrier_semaphore()
    peers = [chip_dev(k) for k in range(1, 8)] + [z_dev(k) for k in range(1, NZ)] + [xl_dev, sib_dev]
    for peer in peers:
        pl.semaphore_signal(barrier, inc=1, device_id=peer, device_id_type=MESH)
    for p in range(2):
        for d in range(2):
            feat_load(p, d).start()
    for load in loads:
        load.start()
    for p in range(2):
        for d in range(2):
            feat_load(p, d).wait()
    pl.semaphore_wait(barrier, len(peers))

    def xg_at(p, h, sub, k, other):
        xx = xh if sub == 1 else 1 - xh
        c = xx * 8 + ((y + k + NY) % NY) * 2 + (1 - core if other else core)
        return xg.at[p, h, pl.ds(pl.multiple_of(c * BLK, BLK), BLK)]

    def ac_places(s):
        return [(e, h) for e in range(2) for h in ((e, 1 - e) if s == 1 else (e,))]

    def ac_sem(e, h, s):
        return 2 * e + h if s == 1 else 4 + e

    def ac_send(p, sub, e, h, s):
        here = xg_at(p, h, sub, (2 * e - 1) * s, False)
        remote(here, here, a_ys.at[p, sub, e], a_yr.at[p, sub, ac_sem(e, h, s + 1)], y_dev(e)).start()

    def ac_cross(p, sub, h, k, i):
        here = xg_at(p, h, sub, k, False)
        remote(here, here, a_ds.at[p, sub], a_dr.at[p, sub, i], sib_dev).start()

    def ac_first(p, sub):
        for e, h in ac_places(1):
            ac_send(p, sub, e, h, 0)

    def ac_start(p):
        ac_first(p, 1)
        for h in range(2):
            here = xg_at(p, h, 1, 0, False)
            remote(here, here, a_xs.at[p, h], a_xr.at[p, h], xh_dev).start()
        for h in range(2):
            ac_cross(p, 1, h, 0, h)

    def ac_event(p, i):
        sub, s = ((1, 1), (0, 0), (1, 2), (0, 1), (0, 2))[i]
        if s == 0:
            for h in range(2):
                here = xg_at(p, h, 0, 0, False)
                remote(here, here, a_xs.at[p, h], a_xr.at[p, h], xh_dev).wait_recv()
            ac_first(p, 0)
            for h in range(2):
                ac_cross(p, 0, h, 0, h)
            return
        for e, h in ac_places(s):
            k = (2 * e - 1) * s
            here = xg_at(p, h, sub, k, False)
            remote(here, here, a_ys.at[p, sub, e], a_yr.at[p, sub, ac_sem(e, h, s)], y_dev(e)).wait_recv()
            if s == 1 and h == e:
                ac_send(p, sub, e, h, 1)
            ac_cross(p, sub, h, k, 2 + ac_sem(e, h, s))

    def ac_finish(p):
        for sub in (1, 0):
            for h in range(2):
                here = xg_at(p, h, sub, 0, True)
                remote(here, here, a_ds.at[p, sub], a_dr.at[p, sub, h], sib_dev).wait_recv()
            for s in (1, 2):
                for e, h in ac_places(s):
                    here = xg_at(p, h, sub, (2 * e - 1) * s, True)
                    remote(here, here, a_ds.at[p, sub], a_dr.at[p, sub, 2 + ac_sem(e, h, s)], sib_dev).wait_recv()

    def lay(table, first, step):
        for i in range(16):
            strip[:, i * BLK:(i + 1) * BLK] = table[slot_of[first + i * step]]

    def times(source):
        return jnp.dot(strip[...], source, preferred_element_type=F32)

    class Ring:
        def __init__(self, reach, subs, term, ring_dev, terms, held, send, recv, cross=None):
            self.reach, self.subs, self.term, self.ring_dev = reach, subs, term, ring_dev
            self.terms, self.held, self.send, self.recv, self.cross = terms, held, send, recv, cross

        def split(self, q, s):
            e, sub = q // self.subs, q % self.subs
            return e, sub, (1 - 2 * e) * (self.reach - s), ((e,) if s == 0 else (e, 1 - e))

        def other(self, s):
            out, into, send, recv, dev = self.cross

            def one(q, inner):
                e, sub, k, hs = self.split(q, s)
                for h, value in zip(hs, self.term(False, e, sub, k, hs)):
                    out[q, h, s] = value.astype(BF)
                    remote(out.at[q, h, s], into.at[q, h, s], send.at[q], recv.at[q, h, s], dev).start()
                return inner

            lax.fori_loop(0, 2 * self.subs if s < self.reach else self.subs, one, 0)

        def own(self, s):
            def one(q, inner):
                e, sub, k, hs = self.split(q, s)
                for h, value in zip(hs, self.term(True, e, sub, k, hs)):
                    self.terms[q, h] = value
                return inner

            lax.fori_loop(0, 2 * self.subs, one, 0)

        def add_cross(self, q, h, s):
            if self.cross is None:
                return 0.0
            into, send, recv, dev = self.cross[1:]
            remote(into.at[q, h, s], into.at[q, h, s], send.at[q], recv.at[q, h, s], dev).wait_recv()
            return into[q, h, s].astype(F32)

        def add_ring(self, e, q, h, s):
            here = self.held.at[q, h, s]
            remote(here, here, self.send.at[q], self.recv.at[q, h, s - 1], self.ring_dev(e)).wait_recv()
            return self.held[q, h, s].astype(F32)

        def step(self, s):
            def one(q, inner):
                e, sub, k, hs = self.split(q, s)
                for i, h in enumerate(hs):
                    value = self.terms[q, h] + self.add_cross(q, h, s)
                    if s > i:
                        value = value + self.add_ring(e, q, h, s)
                    self.held[q, h, s] = value.astype(BF)
                    remote(self.held.at[q, h, s], self.held.at[q, h, s + 1], self.send.at[q],
                           self.recv.at[q, h, s], self.ring_dev(e)).start()
                return inner

            lax.fori_loop(0, 2 * self.subs, one, 0)

        def last_own(self, sums):
            def one(sub, inner):
                for h, value in zip((0, 1), self.term(True, 0, sub, 0, (0, 1))):
                    sums[sub, h] = value
                return inner

            lax.fori_loop(0, self.subs, one, 0)

        def last(self, sums, sub):
            for h in range(2):
                value = sums[sub, h] + self.add_cross(sub, h, self.reach)
                for e in range(2):
                    value = value + self.add_ring(e, e * self.subs + sub, h, self.reach)
                sums[sub, h] = value

        def drain(self):
            for q in range(2 * self.subs):
                sent = xg.at[0, 0, pl.ds(0, (2 * self.reach - 1) * BLK)]
                remote(sent, sent, self.send.at[q], self.recv.at[q, 0, 0], self.ring_dev(0)).wait_send()
                if self.cross is not None:
                    send, recv, dev = self.cross[2:]
                    count = 2 * self.reach - 1 + (2 if q < self.subs else 0)
                    sent = xg.at[0, 0, pl.ds(0, count * BLK)]
                    remote(sent, sent, send.at[q], recv.at[q, 0, 0], dev).wait_send()

    def z_ring_dev(e):
        return z_dev(1 - 2 * e)

    def row_term_0(mine, e, sub, k, hs):
        xd = xl + (1 - sub) * (1 - 2 * xl)
        lay(tiles, (xd * NZ + (z + k + NZ) % NZ) * 16, 1)
        return [times(xg[0, h]) for h in hs]

    row_a = Ring(NZ // 2, 2, row_term_0, z_ring_dev, part.at[0], rr, b_s, b_r)

    def row_term_1(mine, e, sub, k, hs):
        lay(tiles, ((xl if mine else 1 - xl) * NZ + (z + k + NZ) % NZ) * 16, 1)
        return [times(xg[1, h]) for h in hs]

    row_b = Ring(NZ // 2, 1, row_term_1, z_ring_dev, part.at[1], rb, n_s, n_r, (rbs, rbr, nx_s, nx_r, xl_dev))

    def row_send():
        row_a.last(fin.at[0], 0)
        for h in range(2):
            rrs[h] = fin[0, 0, h].astype(BF)
            remote(rrs.at[h], rrx.at[h], bx_s.at[h], bx_r.at[h], xl_dev).start()
        row_a.last(fin.at[0], 1)

    def row_finish(p):
        for h in range(2):
            if p == 0:
                remote(rrx.at[h], rrx.at[h], bx_s.at[h], bx_r.at[h], xl_dev).wait_recv()
                zq[h] = (fin[0, 1, h] + rrx[h].astype(F32)).astype(BF)
            else:
                zq[2 + h] = fin[1, 0, h].astype(BF)
        both = jnp.concatenate([zq[2 * p], zq[2 * p + 1]], axis=1)
        value = jnp.dot(both, weight[pl.ds(p * 512, 512), :], preferred_element_type=F32)
        if p == 0:
            acc[...] = value
        else:
            acc[...] = acc[...] + value

    own_h = pl.ds(pl.multiple_of(row * BLK, BLK), BLK)

    def activate(p):
        for d in range(2):
            lanes = slice((2 * p + d) * QUART, (2 * p + d + 1) * QUART)
            hidden = acc[:, lanes]
            sig = 1.0 / (1.0 + jnp.exp(-hidden))
            act[:, lanes] = (hidden * sig).astype(BF)
            slope = sig * (1.0 + hidden * (1.0 - sig))
            hg[p, d, own_h, :] = (cot[:, lanes].astype(F32) * slope).astype(BF)

    def hg_at(p, h, sub, k):
        xx = xl if sub == 1 else 1 - xl
        return hg.at[p, h, pl.ds(pl.multiple_of((xx * NZ + (z + k + NZ) % NZ) * BLK, BLK), BLK)]

    def ag_places(s):
        return [(e, h) for e in range(2) for h in (e, 1 - e) if s <= NZ // 2 - (h != e)]

    def ag_send(p, sub, e, h, s):
        here = hg_at(p, h, sub, (2 * e - 1) * s)
        remote(here, here, c_s.at[p, sub, e], c_r.at[p, sub, 2 * e + h, s], z_ring_dev(e)).start()

    def ag_cross(p, h, k, i):
        here = hg_at(p, h, 1, k)
        remote(here, here, cx_s.at[p], cx_r.at[p, i], xl_dev).start()

    def ag_cross_wait(p, h, k, i):
        here = hg_at(p, h, 0, k)
        remote(here, here, cx_s.at[p], cx_r.at[p, i], xl_dev).wait_recv()

    def ag_start(p):
        for e, h in ag_places(1):
            ag_send(p, 1, e, h, 0)
        for h in range(2):
            ag_cross(p, h, 0, h)

    def ag_partner(p):
        for h in range(2):
            ag_cross_wait(p, h, 0, h)
        if p == 0:
            for e, h in ag_places(1):
                ag_send(p, 0, e, h, 0)
        else:
            for s in range(1, NZ // 2 + 1):
                for e, h in ag_places(s):
                    ag_cross_wait(p, h, (2 * e - 1) * s, 4 * s + 2 * e + h - 2)

    def ag_step(p, sub, s):
        for e, h in ag_places(s):
            k = (2 * e - 1) * s
            here = hg_at(p, h, sub, k)
            remote(here, here, c_s.at[p, sub, e], c_r.at[p, sub, 2 * e + h, s - 1], z_ring_dev(e)).wait_recv()
            if (e, h) in ag_places(s + 1):
                ag_send(p, sub, e, h, s)
            if p == 1:
                ag_cross(p, h, k, 4 * s + 2 * e + h - 2)

    def col_place(sub, k):
        return (xh + (1 - sub) * (1 - 2 * xh)) * NY + (y + k + NY) % NY

    def col_ring(p):
        def term(mine, e, sub, k, hs):
            lay(tiles_t, col_place(sub, k) * 2 + (core if mine else 1 - core), 16)
            return [times(hg[p, h]) for h in hs]

        return Ring(NY // 2, 2, term, y_dev, part.at[p], rc.at[p], e_s.at[p], e_r.at[p],
                    (rcs.at[p], rcr.at[p], ed_s.at[p], ed_r.at[p], sib_dev))

    cols = [col_ring(0), col_ring(1)]

    def col_send(p):
        cols[p].last(fin.at[p], 0)
        for h in range(2):
            rcf[p, h] = fin[p, 0, h].astype(BF)
            remote(rcf.at[p, h], rcx.at[p, h], ex_s.at[p, h], ex_r.at[p, h], xh_dev).start()
        cols[p].last(fin.at[p], 1)

    def col_finish(p):
        delta = []
        for h in range(2):
            remote(rcx.at[p, h], rcx.at[p, h], ex_s.at[p, h], ex_r.at[p, h], xh_dev).wait_recv()
            delta.append((fin[p, 1, h] + rcx[p, h].astype(F32)).astype(BF))
        value = lax.dot_general(
            jnp.concatenate(delta, axis=1), weight[:, pl.ds(p * 512, 512)],
            (((1,), (1,)), ((), ())), preferred_element_type=F32,
        )
        if p == 0:
            acc[...] = value
        else:
            fgrad[...] = (acc[...] + value).astype(BF)

    def turn_z():
        for k in range(8):
            zt[k] = zq[k // 2, :, (k % 2) * BLK:(k % 2 + 1) * BLK].T

    def wt_term(mine, e, sub, k, hs):
        tile = zt[col_place(sub, k)]
        side = core if mine else 1 - core
        return [jnp.dot(tile, hg[side, h, own_h, :], preferred_element_type=F32) for h in hs]

    wts = Ring(NY // 2, 2, wt_term, y_dev, vpart, vc, v_s, v_r, (vcs, vcr, vd_s, vd_r, sib_dev))

    def wt_send():
        wts.last(vfin, 0)
        for h in range(2):
            vcf[h] = vfin[0, h].astype(BF)
            remote(vcf.at[h], vcx.at[h], vx_s.at[h], vx_r.at[h], xh_dev).start()
        wts.last(vfin, 1)

    def wt_spread():
        for d in range(2):
            remote(vcx.at[d], vcx.at[d], vx_s.at[d], vx_r.at[d], xh_dev).wait_recv()
            value = (vfin[1, d] + vcx[d].astype(F32)).astype(BF)
            for k in range(NZ):
                ws[k, :, d * QUART:(d + 1) * QUART] = value[16 * k:16 * (k + 1), :]
        for k in range(1, NZ):
            remote(ws.at[(z + k) % NZ], wr.at[z], z_s, z_r.at[k], z_dev(k)).start()

    def wt_sum():
        total = ws[z].astype(F32)
        for k in range(1, NZ):
            zz = (z - k + NZ) % NZ
            remote(wr.at[zz], wr.at[zz], z_s, z_r.at[k], z_dev(k)).wait_recv()
            total = total + wr[zz].astype(F32)
        wxs[...] = total.astype(BF)
        remote(wxs, wxr, zx_s, zx_r, xl_dev).start()

    def wout_at(k, zz, side):
        lanes = pl.ds(pl.multiple_of(side * 512, 512), 512)
        return wout.at[k, zz, :, lanes]

    def wt_share():
        remote(wxr, wxr, zx_s, zx_r, xl_dev).wait_recv()
        value = (wxs[...].astype(F32) + wxr[...].astype(F32)).astype(BF)
        wfin[...] = value
        wout[chip, z, :, pl.ds(pl.multiple_of(core * 512, 512), 512)] = value
        for k in range(1, 8):
            remote(wfin, wout_at(chip, z, core), k_s, k_r.at[k], chip_dev(k)).start()

    def wz_at(k, side):
        lanes = pl.ds(pl.multiple_of(side * 512, 512), 512)
        return wout.at[:, (z + k + NZ) % NZ, :, lanes]

    def wz_send(d, s):
        here = wz_at((2 * d - 1) * s, core)
        if s < (NZ // 2 if d == 0 else NZ // 2 - 1):
            remote(here, here, g_s.at[d], g_r.at[d, s], z_dev(1 - 2 * d)).start()
        if s > 0 or d == 0:
            remote(here, here, gd_s, gd_r.at[d, s], sib_dev).start()

    def wz_start():
        for k in range(1, 8):
            there = wout_at((chip - k + 8) % 8, z, core)
            remote(there, there, k_s, k_r.at[k], chip_dev(k)).wait_recv()
        for d in range(2):
            wz_send(d, 0)

    def wz_step(s):
        for d in range(2):
            if s <= (NZ // 2 if d == 0 else NZ // 2 - 1):
                here = wz_at((2 * d - 1) * s, core)
                remote(here, here, g_s.at[d], g_r.at[d, s - 1], z_dev(1 - 2 * d)).wait_recv()
                wz_send(d, s)

    def wz_finish():
        for d in range(2):
            for s in range(NZ // 2 + 1 if d == 0 else NZ // 2):
                if s > 0 or d == 0:
                    here = wz_at((2 * d - 1) * s, 1 - core)
                    remote(here, here, gd_s, gd_r.at[d, s], sib_dev).wait_recv()

    def flip(lo, n):
        def one(t, carry):
            tiles_t[t] = tiles[t].T
            return carry
        lax.fori_loop(lo, lo + n, one, 0)

    ac_start(0)
    ac_start(1)
    loads[0].wait()
    tiles[64] = jnp.zeros((BLK, BLK), BF)
    tiles_t[64] = jnp.zeros((BLK, BLK), BF)
    ac_event(0, 0)
    ac_event(0, 1)
    ac_event(1, 0)
    ac_event(0, 2)
    ac_event(1, 1)
    ac_event(0, 3)
    ac_event(1, 2)
    ac_event(0, 4)
    ac_event(1, 3)
    ac_finish(0)
    row_a.own(0)
    row_a.step(0)
    ac_event(1, 4)
    ac_finish(1)
    loads[1].wait()
    loads[2].wait()
    row_b.other(0)
    row_a.own(1)
    row_b.other(1)
    row_b.own(0)
    row_a.step(1)
    row_b.step(0)
    flip(0, 20)
    for s in range(1, NZ // 2):
        if s < NZ // 2 - 1:
            row_a.own(s + 1)
            row_b.other(s + 1)
        else:
            row_a.last_own(fin.at[0])
            row_b.other(s + 1)
        row_b.own(s)
        if s < NZ // 2 - 1:
            row_a.step(s + 1)
        else:
            row_send()
        row_b.step(s)
        if s < NZ // 2 - 1:
            flip(20 * s, 20)
    row_b.last_own(fin.at[1])
    flip(60, 4)
    row_finish(0)
    row_b.last(fin.at[1], 0)
    row_finish(1)
    activate(0)
    ag_start(0)
    activate(1)
    act_store = pltpu.make_async_copy(act, act_out, store_sem.at[0])
    act_store.start()
    ag_start(1)
    ag_partner(0)
    turn_z()
    wts.other(0)
    wts.own(0)
    for s in range(1, NZ // 2 + 1):
        ag_step(0, 1, s)
        if s == 1:
            wts.step(0)
            wts.other(1)
            wts.own(1)
        if s == 2:
            wt_send()
        ag_step(1, 1, s)
        if s == 1:
            wts.step(1)
            wts.other(2)
            wts.last_own(vfin)
        if s == 2:
            wt_spread()
        ag_step(0, 0, s)
        if s == 3:
            wt_sum()
    wt_share()
    cols[0].other(0)
    cols[0].own(0)
    wz_start()
    ag_partner(1)
    cols[1].other(0)
    cols[1].own(0)
    cols[0].step(0)
    cols[0].other(1)
    cols[0].own(1)
    cols[1].step(0)
    wz_step(1)
    cols[1].other(1)
    cols[1].own(1)
    cols[0].step(1)
    cols[0].other(2)
    cols[0].last_own(fin.at[0])
    cols[1].step(1)
    wz_step(2)
    cols[1].other(2)
    cols[1].last_own(fin.at[1])
    col_send(0)
    wz_step(3)
    col_send(1)
    col_finish(0)
    wz_step(4)
    col_finish(1)
    fgrad_store = pltpu.make_async_copy(fgrad, fgrad_out, store_sem.at[1])
    fgrad_store.start()
    wz_finish()
    wout_store = pltpu.make_async_copy(wout, wout_out, store_sem.at[2])
    wout_store.start()
    fgrad_store.wait()
    wout_store.wait()
    act_store.wait()

    for p in range(2):
        for sub in range(2):
            for e in range(2):
                sent = xg.at[0, 0, pl.ds(0, 3 * BLK)]
                remote(sent, sent, a_ys.at[p, sub, e], a_yr.at[p, sub, 0], y_dev(e)).wait_send()
                if (p == 0 or sub == 1):
                    sent = hg.at[0, 0, pl.ds(0, 7 * BLK)]
                    remote(sent, sent, c_s.at[p, sub, e], c_r.at[p, sub, 0, 0], z_dev(1)).wait_send()
            sent = xg.at[0, 0, pl.ds(0, 8 * BLK)]
            remote(sent, sent, a_ds.at[p, sub], a_dr.at[p, sub, 0], sib_dev).wait_send()
        for h in range(2):
            sent = xg.at[0, 0, pl.ds(0, BLK)]
            remote(sent, sent, a_xs.at[p, h], a_xr.at[p, h], xh_dev).wait_send()
            remote(rcx.at[p, h], rcx.at[p, h], ex_s.at[p, h], ex_r.at[p, h], xh_dev).wait_send()
        sent = hg.at[0, 0, pl.ds(0, (16 if p else 2) * BLK)]
        remote(sent, sent, cx_s.at[p], cx_r.at[p, 0], xl_dev).wait_send()
        cols[p].drain()
    row_a.drain()
    row_b.drain()
    for h in range(2):
        remote(rrx.at[h], rrx.at[h], bx_s.at[h], bx_r.at[h], xl_dev).wait_send()
    wts.drain()
    for h in range(2):
        remote(vcx.at[h], vcx.at[h], vx_s.at[h], vx_r.at[h], xh_dev).wait_send()
    sent = wr.at[pl.ds(0, 7)]
    remote(sent, sent, z_s, z_r.at[1], z_dev(1)).wait_send()
    sent = wr.at[pl.ds(0, 7)]
    remote(sent, sent, k_s, k_r.at[1], chip_dev(1)).wait_send()
    remote(wxs, wxs, zx_s, zx_r, xl_dev).wait_send()
    for d in range(2):
        sent = wout.at[:, pl.ds(0, NZ // 2 - d), :, pl.ds(0, 512)]
        remote(sent, sent, g_s.at[d], g_r.at[d, 0], z_dev(1)).wait_send()
    sent = wout.at[:, :, :, pl.ds(0, 512)]
    remote(sent, sent, gd_s, gd_r.at[0, 0], sib_dev).wait_send()


def layer(slot_of, features, weight, cotangent, tiles):
    hbm = pl.BlockSpec(memory_space=pl.ANY)
    dma = pltpu.SemaphoreType.DMA
    chunk = (BLK, QUART)
    return pl.pallas_call(
        kernel,
        name="layer",
        out_shape=(
            jax.ShapeDtypeStruct((BLK, 1024), BF),
            jax.ShapeDtypeStruct((BLK, 1024), BF),
            jax.ShapeDtypeStruct((8, NZ, 16, 1024), BF),
        ),
        in_specs=[pl.BlockSpec(memory_space=pltpu.SMEM)] + [hbm] * 4,
        out_specs=(hbm, hbm, hbm),
        scratch_shapes=[
            pltpu.VMEM((1024, 1024), BF),
            pltpu.VMEM((BLK, 1024), BF),
            pltpu.VMEM((BLK, 1024), BF),
            pltpu.VMEM((BLK, 1024), BF),
            pltpu.VMEM((8, NZ, 16, 1024), BF),
            pltpu.VMEM((2, 2, 2048, QUART), BF),
            pltpu.VMEM((2, 2, 2048, QUART), BF),
            pltpu.VMEM((65, BLK, BLK), BF),
            pltpu.VMEM((65, BLK, BLK), BF),
            pltpu.VMEM((BLK, 2048), BF),
            pltpu.VMEM((BLK, 1024), F32),
            pltpu.VMEM((4, *chunk), BF),
            pltpu.VMEM((8, BLK, BLK), BF),
            pltpu.VMEM((2, 4, 2, *chunk), F32),
            pltpu.VMEM((2, 2, 2, *chunk), F32),
            pltpu.VMEM((4, 2, 5, *chunk), BF),
            pltpu.VMEM((2, *chunk), BF),
            pltpu.VMEM((2, *chunk), BF),
            pltpu.VMEM((2, 2, 5, *chunk), BF),
            pltpu.VMEM((2, 2, 5, *chunk), BF),
            pltpu.VMEM((2, 2, 5, *chunk), BF),
            pltpu.VMEM((2, 4, 2, 3, *chunk), BF),
            pltpu.VMEM((2, 4, 2, 3, *chunk), BF),
            pltpu.VMEM((2, 4, 2, 3, *chunk), BF),
            pltpu.VMEM((2, 2, *chunk), BF),
            pltpu.VMEM((2, 2, *chunk), BF),
            pltpu.VMEM((4, 2, *chunk), F32),
            pltpu.VMEM((2, 2, *chunk), F32),
            pltpu.VMEM((4, 2, 3, *chunk), BF),
            pltpu.VMEM((4, 2, 3, *chunk), BF),
            pltpu.VMEM((4, 2, 3, *chunk), BF),
            pltpu.VMEM((2, *chunk), BF),
            pltpu.VMEM((2, *chunk), BF),
            pltpu.VMEM((NZ, 16, 512), BF),
            pltpu.VMEM((NZ, 16, 512), BF),
            pltpu.VMEM((16, 512), BF),
            pltpu.VMEM((16, 512), BF),
            pltpu.VMEM((16, 512), BF),
            dma((3,)), dma((2, 2)), dma((3,)),
            dma((2, 2, 2)), dma((2, 2, 6)), dma((2, 2)), dma((2, 2)), dma((2, 2)), dma((2, 2, 8)),
            dma((4,)), dma((4, 2, 4)), dma((2,)), dma((2,)), dma((2,)), dma((2, 2, 4)), dma((2,)), dma((2, 2, 5)),
            dma((2, 2, 2)), dma((2, 2, 4, 4)), dma((2,)), dma((2, 18)),
            dma((2, 4)), dma((2, 4, 2, 2)), dma((2, 2)), dma((2, 2)), dma((2, 4)), dma((2, 4, 2, 3)),
            dma((4,)), dma((4, 2, 2)), dma((2,)), dma((2,)), dma((4,)), dma((4, 2, 3)),
            dma, dma((NZ,)), dma, dma, dma, dma((NZ,)), dma((2,)), dma((2, 4)), dma, dma((2, 5)),
        ],
        compiler_params=pltpu.CompilerParams(
            collective_id=0, has_side_effects=True, vmem_limit_bytes=60 * 1024 * 1024,
        ),
    )(slot_of, features, weight, cotangent, tiles)


def on_device(features, weight, cotangent, tile_values, block_row, block_column, tile_count):
    slots = jnp.arange(64, dtype=jnp.int32)
    cell = block_row[0, 0] * 16 + block_column[0, 0]
    cell = jnp.where(slots < tile_count[0, 0], cell, -1)
    named = cell[None, :] == jnp.arange(256, dtype=jnp.int32)[:, None]
    slot_of = jnp.min(jnp.where(named, slots[None, :], 64), axis=1)
    activated, feat_grad, pieces = layer(slot_of, features, weight, cotangent, tile_values[0, 0])
    weight_grad = pieces.reshape(1024, 1024).astype(F32) * 32768 ** (-0.5)
    return activated, feat_grad, weight_grad


def solution(mesh):
    return jax.shard_map(
        on_device,
        mesh=mesh,
        in_specs=(
            P(("row", "col"), None),
            P(),
            P(("col", "row"), None),
            P("row", "col", None, None, None),
            P("row", "col", None),
            P("row", "col", None),
            P("row", "col"),
        ),
        out_specs=(P(("col", "row"), None), P(("row", "col"), None), P()),
        check_vma=False,
    )
```

time: 162 us -> 150 us (0.926)
  Pallas kernels: 153 us -> 141 us
    pallas_call x1, Pallas kernels: 153 us -> 141 us  [layer(): pl.pallas_call(kernel, name='layer', out_shape=(jax.ShapeDtypeStruct((BLK...]
where the time goes in v3:
time: 150 us; the launch traced here: 149 us
  Pallas kernels  141 us (94%)
  other arithmetic  5.65 us (4%)
    pallas_call x1, Pallas kernels, layer(): pl.pallas_call(kernel, name='layer', out_shape=(jax.ShapeDtypeStruct((BLK...  141 us
    mul x1, other arithmetic, on_device(): weight_grad = pieces.reshape(1024, 1024).astype(F32) * 32768 ** (-0.5)  4.32 us

profile of v3, /device:TPU:1, one launch (start us, length us, event | category | flops | bytes accessed | tf_op | source)
XLA Modules:
  0.0 149.4 jit_solution(2056113635111539306)
XLA Ops:
  1.3 0.7 compare_select_fusion
  2.0 0.7 select_reduce_fusion.slot_of
  2.6 141.0 %layer.1 = (bf16[128,1024]{1,0:T(8,128)(2,1)}, bf16[128,1024]{1,0:T(8,128)(2,1)}, bf16[8,8,16,1024]{3,2,1,0:T(8,128)(2,1)}) custom-call(s32[256]{0:T(256)} %select_reduce_fusion.slot_of, bf16[128,1024]{1,0:T(8,128)(2,1)} %feat_in.1, bf16[1024,1024]{1,0:T(8,128)(2,1)} %weight_in.1, bf16[128,1024]{1,0:T(8,128)(2,1)} %cot_in.1, bf16[64,128,128]{2,1,0:T(8,128)(2,1)} %bitcast.7), custom_call_target="tpu_custom_call" | custom-call | tf_op jit(solution)/shard_map/layer/pallas_call | solution.py:595
  143.6 0.0 copy-start.1
  143.6 0.0 copy-start
  143.6 4.3 %convert_multiply_fusion = f32[8,8,16,1024]{3,2,1,0:T(8,128)} fusion(bf16[8,8,16,1024]{3,2,1,0:T(8,128)(2,1)} %get-tuple-element.8), kind=kLoop, calls=%fused_computation | loop fusion | flops 2097152 | bytes 6291456 | tf_op jit(solution)/shard_map/mul | solution.py:665
  147.9 0.0 copy-done.1
  147.9 0.7 copy.13
  148.6 0.0 copy-done
  148.6 0.7 copy.14
Async XLA Ops:
  143.6 4.3 %copy-start.1 = (bf16[128,1024]{1,0:T(8,128)(2,1)S(1)}, bf16[128,1024]{1,0:T(8,128)(2,1)}, u32[]{:S(2)}) copy-start(bf16[128,1024]{1,0:T(8,128)(2,1)} %get-tuple-element.12) | copy-start | bytes 786436
  143.6 5.0 %copy-start = (bf16[128,1024]{1,0:T(8,128)(2,1)S(1)}, bf16[128,1024]{1,0:T(8,128)(2,1)}, u32[]{:S(2)}) copy-start(bf16[128,1024]{1,0:T(8,128)(2,1)} %get-tuple-element.13) | copy-start | bytes 786436

commit v4 on v3

--- a/solution.py
+++ b/solution.py
@@ -105,28 +105,41 @@
     def ac_start(p):
         ac_first(p, 1)
         for h in range(2):
-            here = xg_at(p, h, 1, 0, False)
-            remote(here, here, a_xs.at[p, h], a_xr.at[p, h], xh_dev).start()
+            ac_over(p, h, 0, h)
         for h in range(2):
             ac_cross(p, 1, h, 0, h)
+
+    def ac_over(p, h, k, i):
+        here = xg_at(p, h, 1, k, False)
+        remote(here, here, a_xs.at[p], a_xr.at[p, i], xh_dev).start()
+
+    def ac_over_wait(p, h, k, i):
+        here = xg_at(p, h, 0, k, False)
+        remote(here, here, a_xs.at[p], a_xr.at[p, i], xh_dev).wait_recv()
 
     def ac_event(p, i):
         sub, s = ((1, 1), (0, 0), (1, 2), (0, 1), (0, 2))[i]
         if s == 0:
             for h in range(2):
-                here = xg_at(p, h, 0, 0, False)
-                remote(here, here, a_xs.at[p, h], a_xr.at[p, h], xh_dev).wait_recv()
-            ac_first(p, 0)
+                ac_over_wait(p, h, 0, h)
+            if p == 0:
+                ac_first(p, 0)
             for h in range(2):
                 ac_cross(p, 0, h, 0, h)
             return
         for e, h in ac_places(s):
             k = (2 * e - 1) * s
-            here = xg_at(p, h, sub, k, False)
-            remote(here, here, a_ys.at[p, sub, e], a_yr.at[p, sub, ac_sem(e, h, s)], y_dev(e)).wait_recv()
-            if s == 1 and h == e:
-                ac_send(p, sub, e, h, 1)
-            ac_cross(p, sub, h, k, 2 + ac_sem(e, h, s))
+            i = 2 + ac_sem(e, h, s)
+            if p == 1 and sub == 0:
+                ac_over_wait(p, h, k, i)
+            else:
+                here = xg_at(p, h, sub, k, False)
+                remote(here, here, a_ys.at[p, sub, e], a_yr.at[p, sub, i - 2], y_dev(e)).wait_recv()
+                if s == 1 and h == e:
+                    ac_send(p, sub, e, h, 1)
+                if p == 1:
+                    ac_over(p, h, k, i)
+            ac_cross(p, sub, h, k, i)
 
     def ac_finish(p):
         for sub in (1, 0):
@@ -453,16 +466,16 @@
     ac_event(0, 3)
     ac_event(1, 2)
     ac_event(0, 4)
-    ac_event(1, 3)
     ac_finish(0)
     row_a.own(0)
     row_a.step(0)
+    ac_event(1, 3)
+    row_a.own(1)
     ac_event(1, 4)
     ac_finish(1)
     loads[1].wait()
     loads[2].wait()
     row_b.other(0)
-    row_a.own(1)
     row_b.other(1)
     row_b.own(0)
     row_a.step(1)
@@ -507,13 +520,13 @@
         if s == 2:
             wt_send()
         ag_step(1, 1, s)
+        ag_step(0, 0, s)
         if s == 1:
             wts.step(1)
             wts.other(2)
             wts.last_own(vfin)
         if s == 2:
             wt_spread()
-        ag_step(0, 0, s)
         if s == 3:
             wt_sum()
     wt_share()
@@ -555,16 +568,17 @@
     for p in range(2):
         for sub in range(2):
             for e in range(2):
-                sent = xg.at[0, 0, pl.ds(0, 3 * BLK)]
-                remote(sent, sent, a_ys.at[p, sub, e], a_yr.at[p, sub, 0], y_dev(e)).wait_send()
+                if (p == 0 or sub == 1):
+                    sent = xg.at[0, 0, pl.ds(0, 3 * BLK)]
+                    remote(sent, sent, a_ys.at[p, sub, e], a_yr.at[p, sub, 0], y_dev(e)).wait_send()
                 if (p == 0 or sub == 1):
                     sent = hg.at[0, 0, pl.ds(0, 7 * BLK)]
                     remote(sent, sent, c_s.at[p, sub, e], c_r.at[p, sub, 0, 0], z_dev(1)).wait_send()
             sent = xg.at[0, 0, pl.ds(0, 8 * BLK)]
             remote(sent, sent, a_ds.at[p, sub], a_dr.at[p, sub, 0], sib_dev).wait_send()
-        for h in range(2):
-            sent = xg.at[0, 0, pl.ds(0, BLK)]
-            remote(sent, sent, a_xs.at[p, h], a_xr.at[p, h], xh_dev).wait_send()
+        sent = xg.at[0, 0, pl.ds(0, (8 if p else 2) * BLK)]
+        remote(sent, sent, a_xs.at[p], a_xr.at[p, 0], xh_dev).wait_send()
+        for h in range(2):
             remote(rcx.at[p, h], rcx.at[p, h], ex_s.at[p, h], ex_r.at[p, h], xh_dev).wait_send()
         sent = hg.at[0, 0, pl.ds(0, (16 if p else 2) * BLK)]
         remote(sent, sent, cx_s.at[p], cx_r.at[p, 0], xl_dev).wait_send()
@@ -642,7 +656,7 @@
             pltpu.VMEM((16, 512), BF),
             pltpu.VMEM((16, 512), BF),
             dma((3,)), dma((2, 2)), dma((3,)),
-            dma((2, 2, 2)), dma((2, 2, 6)), dma((2, 2)), dma((2, 2)), dma((2, 2)), dma((2, 2, 8)),
+            dma((2, 2, 2)), dma((2, 2, 6)), dma((2,)), dma((2, 8)), dma((2, 2)), dma((2, 2, 8)),
             dma((4,)), dma((4, 2, 4)), dma((2,)), dma((2,)), dma((2,)), dma((2, 2, 4)), dma((2,)), dma((2, 2, 5)),
             dma((2, 2, 2)), dma((2, 2, 4, 4)), dma((2,)), dma((2, 18)),
             dma((2, 4)), dma((2, 4, 2, 2)), dma((2, 2)), dma((2, 2)), dma((2, 4)), dma((2, 4, 2, 3)),
@@ -657,10 +671,9 @@
 
 def on_device(features, weight, cotangent, tile_values, block_row, block_column, tile_count):
     slots = jnp.arange(64, dtype=jnp.int32)
-    cell = block_row[0, 0] * 16 + block_column[0, 0]
-    cell = jnp.where(slots < tile_count[0, 0], cell, -1)
-    named = cell[None, :] == jnp.arange(256, dtype=jnp.int32)[:, None]
-    slot_of = jnp.min(jnp.where(named, slots[None, :], 64), axis=1)
+    cells = jnp.arange(256, dtype=jnp.int32)[:, None]
+    named = (block_row[0] == cells // 16) & (block_column[0] == cells % 16) & (slots < tile_count[0, 0])
+    slot_of = jnp.min(jnp.where(named, slots, 64), axis=1)
     activated, feat_grad, pieces = layer(slot_of, features, weight, cotangent, tile_values[0, 0])
     weight_grad = pieces.reshape(1024, 1024).astype(F32) * 32768 ** (-0.5)
     return activated, feat_grad, weight_grad

time: 150 us -> 147 us (0.980)
  Pallas kernels: 141 us -> 138 us
    pallas_call x1, Pallas kernels: 141 us -> 138 us  [layer(): pl.pallas_call(kernel, name='layer', out_shape=(jax.ShapeDtypeStruct((BLK...]
where the time goes in v4:
time: 147 us
  Pallas kernels  138 us (94%)
  other arithmetic  5.67 us (4%)
    pallas_call x1, Pallas kernels, layer(): pl.pallas_call(kernel, name='layer', out_shape=(jax.ShapeDtypeStruct((BLK...  138 us
    mul x1, other arithmetic, on_device(): weight_grad = pieces.reshape(1024, 1024).astype(F32) * 32768 ** (-0.5)  4.32 us

profile of v4, /device:TPU:1, one launch (start us, length us, event | category | flops | bytes accessed | tf_op | source)
XLA Modules:
  0.0 146.5 jit_solution(3337669346981633628)
XLA Ops:
  1.3 1.3 select_reduce_fusion.slot_of
  2.6 138.1 %layer.1 = (bf16[128,1024]{1,0:T(8,128)(2,1)}, bf16[128,1024]{1,0:T(8,128)(2,1)}, bf16[8,8,16,1024]{3,2,1,0:T(8,128)(2,1)}) custom-call(s32[256]{0:T(256)} %select_reduce_fusion.slot_of, bf16[128,1024]{1,0:T(8,128)(2,1)} %feat_in.1, bf16[1024,1024]{1,0:T(8,128)(2,1)} %weight_in.1, bf16[128,1024]{1,0:T(8,128)(2,1)} %cot_in.1, bf16[64,128,128]{2,1,0:T(8,128)(2,1)} %bitcast.7), custom_call_target="tpu_custom_call" | custom-call | tf_op jit(solution)/shard_map/layer/pallas_call | solution.py:609
  140.8 0.0 copy-start.1
  140.8 0.0 copy-start
  140.8 4.3 %convert_multiply_fusion = f32[8,8,16,1024]{3,2,1,0:T(8,128)} fusion(bf16[8,8,16,1024]{3,2,1,0:T(8,128)(2,1)} %get-tuple-element.8), kind=kLoop, calls=%fused_computation | loop fusion | flops 2097152 | bytes 6291456 | tf_op jit(solution)/shard_map/mul | solution.py:678
  145.1 0.0 copy-done.1
  145.1 0.7 copy.13
  145.8 0.0 copy-done
  145.8 0.7 copy.14
  (2 shorter events, 0.0 us)
Async XLA Ops:
  140.8 4.3 %copy-start.1 = (bf16[128,1024]{1,0:T(8,128)(2,1)S(1)}, bf16[128,1024]{1,0:T(8,128)(2,1)}, u32[]{:S(2)}) copy-start(bf16[128,1024]{1,0:T(8,128)(2,1)} %get-tuple-element.14) | copy-start | bytes 786436
  140.8 5.0 %copy-start = (bf16[128,1024]{1,0:T(8,128)(2,1)S(1)}, bf16[128,1024]{1,0:T(8,128)(2,1)}, u32[]{:S(2)}) copy-start(bf16[128,1024]{1,0:T(8,128)(2,1)} %get-tuple-element.15) | copy-start | bytes 786436

commit v5 on v4

--- a/solution.py
+++ b/solution.py
@@ -555,12 +555,12 @@
     col_send(1)
     col_finish(0)
     wz_step(4)
+    wz_finish()
+    wout_store = pltpu.make_async_copy(wout, wout_out, store_sem.at[2])
+    wout_store.start()
     col_finish(1)
     fgrad_store = pltpu.make_async_copy(fgrad, fgrad_out, store_sem.at[1])
     fgrad_store.start()
-    wz_finish()
-    wout_store = pltpu.make_async_copy(wout, wout_out, store_sem.at[2])
-    wout_store.start()
     fgrad_store.wait()
     wout_store.wait()
     act_store.wait()

time: 147 us -> 147 us (level)
  no operation moved by 1% of the time
where the time goes in v5:
time: 147 us
  Pallas kernels  138 us (94%)
  other arithmetic  5.67 us (4%)
    pallas_call x1, Pallas kernels, layer(): pl.pallas_call(kernel, name='layer', out_shape=(jax.ShapeDtypeStruct((BLK...  138 us
    mul x1, other arithmetic, on_device(): weight_grad = pieces.reshape(1024, 1024).astype(F32) * 32768 ** (-0.5)  4.32 us

profile of v5, /device:TPU:1, one launch (start us, length us, event | category | flops | bytes accessed | tf_op | source)
XLA Modules:
  0.0 146.6 jit_solution(10949359759483163340)
XLA Ops:
  1.3 1.3 select_reduce_fusion.slot_of
  2.6 138.2 %layer.1 = (bf16[128,1024]{1,0:T(8,128)(2,1)}, bf16[128,1024]{1,0:T(8,128)(2,1)}, bf16[8,8,16,1024]{3,2,1,0:T(8,128)(2,1)}) custom-call(s32[256]{0:T(256)} %select_reduce_fusion.slot_of, bf16[128,1024]{1,0:T(8,128)(2,1)} %feat_in.1, bf16[1024,1024]{1,0:T(8,128)(2,1)} %weight_in.1, bf16[128,1024]{1,0:T(8,128)(2,1)} %cot_in.1, bf16[64,128,128]{2,1,0:T(8,128)(2,1)} %bitcast.7), custom_call_target="tpu_custom_call" | custom-call | tf_op jit(solution)/shard_map/layer/pallas_call | solution.py:609
  140.9 0.0 copy-start.1
  140.9 0.0 copy-start
  140.9 4.3 %convert_multiply_fusion = f32[8,8,16,1024]{3,2,1,0:T(8,128)} fusion(bf16[8,8,16,1024]{3,2,1,0:T(8,128)(2,1)} %get-tuple-element.8), kind=kLoop, calls=%fused_computation | loop fusion | flops 2097152 | bytes 6291456 | tf_op jit(solution)/shard_map/mul | solution.py:678
  145.2 0.0 copy-done.1
  145.2 0.7 copy.13
  145.9 0.0 copy-done
  145.9 0.7 copy.14
  (2 shorter events, 0.0 us)
Async XLA Ops:
  140.9 4.3 %copy-start.1 = (bf16[128,1024]{1,0:T(8,128)(2,1)S(1)}, bf16[128,1024]{1,0:T(8,128)(2,1)}, u32[]{:S(2)}) copy-start(bf16[128,1024]{1,0:T(8,128)(2,1)} %get-tuple-element.14) | copy-start | bytes 786436
  140.9 5.0 %copy-start = (bf16[128,1024]{1,0:T(8,128)(2,1)S(1)}, bf16[128,1024]{1,0:T(8,128)(2,1)}, u32[]{:S(2)}) copy-start(bf16[128,1024]{1,0:T(8,128)(2,1)} %get-tuple-element.15) | copy-start | bytes 786436
